TPU v7x, 256 devices: a whole 4x4x8 slice. The times are simulated.
256 devices in a mesh: view: 4 (over y_hi, core), row: 8 (over z), col: 8 (over y_lo, x).
Axes of the slice: x: 4, y: 4 (y_hi: 2, y_lo: 2; y = y_hi * 2 + y_lo), z: 8, core: 2. Of those that a mesh axis runs over, the one named last changes fastest.
Arguments:
- view_maps: bfloat16 [16, 32, 128, 768], P('view', 'row', 'col'), may hold values from -6 to 6
- gain_spatial: float32 [768], replicated, may hold values from 0.1 to 1.9
- spatial_query: bfloat16 [768, 768], replicated, may hold values from -8 to 8
- spatial_key: bfloat16 [768, 768], replicated, may hold values from -8 to 8
- spatial_value: bfloat16 [768, 768], replicated, may hold values from -0.21875 to 0.21875
- spatial_output: bfloat16 [768, 768], replicated, may hold values from -0.21875 to 0.21875
- gain_temporal: float32 [768], replicated, may hold values from 0.1 to 1.9
- temporal_query: bfloat16 [768, 768], replicated, may hold values from -8 to 8
- temporal_key: bfloat16 [768, 768], replicated, may hold values from -8 to 8
- temporal_value: bfloat16 [768, 768], replicated, may hold values from -0.21875 to 0.21875
- temporal_output: bfloat16 [768, 768], replicated, may hold values from -0.21875 to 0.21875
Outputs:
- refined: bfloat16 [16, 32, 128, 768], P('view', 'row', 'col')
All inputs are finite; a program needn't handle non-finite values.
Results may differ from a plain program's by a relative error of at most 0.012.
Values may be sent and summed in bfloat16 or wider, within the bound.
No kernel may reach another device: no remote copies, remote signals or barrier semaphores. Data moves between devices by JAX's collectives and lax.ppermute only.
A program may use at most 64 MiB of HBM per device.

v0:
```python
import jax
import jax.numpy as jnp
from jax import lax
from jax.sharding import PartitionSpec as P

HEADS = 12
HEAD_DIM = 64
RADIUS = 3


epsilon = 1e-06
very_negative = -1e30


def padded(block, sides, width):
    for axis, dim in sides:
        count = lax.axis_size(axis)
        forward = [(i, i + 1) for i in range(count - 1)]
        backward = [(target, source) for source, target in forward]
        low = lax.ppermute(
            lax.slice_in_dim(block, block.shape[dim] - width, None, axis=dim), axis, forward
        )
        high = lax.ppermute(lax.slice_in_dim(block, 0, width, axis=dim), axis, backward)
        block = jnp.concatenate([low, block, high], axis=dim)
    return block


def rms_norm(tokens, gain_vector):
    values = tokens.astype(jnp.float32)
    scaled = values * lax.rsqrt(jnp.mean(values * values, axis=-1, keepdims=True) + epsilon)
    return (scaled * gain_vector).astype(jnp.bfloat16)


def project(tokens, weight_matrix):
    flat = tokens.reshape(-1, tokens.shape[-1])
    result = jnp.dot(flat, weight_matrix, preferred_element_type=jnp.float32)
    return result.reshape(tokens.shape[:-1] + (weight_matrix.shape[1],))


def grid_rows(count_rows, count_cols):
    return jnp.broadcast_to(
        jnp.arange(count_rows, dtype=jnp.int32)[:, None], (count_rows, count_cols)
    ).reshape(-1)


def grid_cols(count_rows, count_cols):
    return jnp.broadcast_to(
        jnp.arange(count_cols, dtype=jnp.int32)[None, :], (count_rows, count_cols)
    ).reshape(-1)


def neighbour(queries, keys_wide, values_wide, first_row, first_col, total_rows, total_cols):
    local_views, height, width, features = queries.shape
    wide_rows, wide_cols = (keys_wide.shape[1], keys_wide.shape[2])
    factor = HEAD_DIM ** (-0.5)
    query_rows = grid_rows(height, width)
    query_cols = grid_cols(height, width)
    key_rows = grid_rows(wide_rows, wide_cols)
    key_cols = grid_cols(wide_rows, wide_cols)
    row_gap = key_rows[None, :] - RADIUS - query_rows[:, None]
    col_gap = key_cols[None, :] - RADIUS - query_cols[:, None]
    in_band = (jnp.abs(row_gap) <= RADIUS) & (jnp.abs(col_gap) <= RADIUS)
    global_rows = first_row - RADIUS + key_rows
    global_cols = first_col - RADIUS + key_cols
    inside = (
        (global_rows >= 0)
        & (global_rows < total_rows)
        & (global_cols >= 0)
        & (global_cols < total_cols)
    )
    allowed = (in_band & inside[None, :])[None, :, :]

    def one_view(items):
        query_heads = items[0].reshape(height * width, HEADS, HEAD_DIM)
        key_heads = items[1].reshape(wide_rows * wide_cols, HEADS, HEAD_DIM)
        value_heads = items[2].reshape(wide_rows * wide_cols, HEADS, HEAD_DIM).astype(jnp.float32)
        scores = (
            jnp.einsum("qhe,khe->hqk", query_heads, key_heads, preferred_element_type=jnp.float32)
            * factor
        )
        scores = jnp.where(allowed, scores, very_negative)
        highest = jnp.max(scores, axis=-1, keepdims=True)
        weights = jnp.exp(scores - highest)
        weights = weights / jnp.sum(weights, axis=-1, keepdims=True)
        mixed = jnp.einsum("hqk,khe->qhe", weights, value_heads, precision=lax.Precision.HIGHEST)
        return mixed.reshape(height, width, features).astype(jnp.bfloat16)

    return lax.map(one_view, (queries, keys_wide, values_wide))


def body(
    view_maps,
    gain_spatial,
    spatial_query,
    spatial_key,
    spatial_value,
    spatial_output,
    gain_temporal,
    temporal_query,
    temporal_key,
    temporal_value,
    temporal_output,
):
    local_views, tile_rows, tile_cols = (view_maps.shape[0], view_maps.shape[1], view_maps.shape[2])
    total_rows = lax.axis_size("row") * tile_rows
    total_cols = lax.axis_size("col") * tile_cols
    first_row = lax.axis_index("row") * tile_rows
    first_col = lax.axis_index("col") * tile_cols
    normed = rms_norm(view_maps, gain_spatial)
    queries = project(normed, spatial_query).astype(jnp.bfloat16)
    keys = project(normed, spatial_key).astype(jnp.bfloat16)
    values = project(normed, spatial_value).astype(jnp.bfloat16)
    stacked = jnp.stack([keys, values], 0)
    widened = padded(stacked, (("row", 2), ("col", 3)), RADIUS)
    keys_wide = widened[0]
    values_wide = widened[1]
    attended = neighbour(
        queries, keys_wide, values_wide, first_row, first_col, total_rows, total_cols
    )
    middle = (view_maps.astype(jnp.float32) + project(attended, spatial_output)).astype(
        jnp.bfloat16
    )
    normed_time = rms_norm(middle, gain_temporal)
    factor = HEAD_DIM ** (-0.5)
    positions = tile_rows * tile_cols
    query_time = project(normed_time, temporal_query).astype(jnp.bfloat16)
    key_time = project(normed_time, temporal_key).astype(jnp.bfloat16)
    value_time = project(normed_time, temporal_value).astype(jnp.bfloat16)
    query_heads = query_time.reshape(local_views, positions, HEADS, HEAD_DIM)
    running_max = jnp.full((local_views, positions, HEADS), very_negative, jnp.float32)
    key_heads = lax.all_gather(key_time, "view", axis=0, tiled=True).reshape(
        -1, positions, HEADS, HEAD_DIM
    )
    value_heads = (
        lax.all_gather(value_time, "view", axis=0, tiled=True)
        .reshape(-1, positions, HEADS, HEAD_DIM)
        .astype(jnp.float32)
    )
    scores = (
        jnp.einsum("qphe,kphe->qkph", query_heads, key_heads, preferred_element_type=jnp.float32)
        * factor
    )
    new_max = jnp.maximum(running_max, jnp.max(scores, axis=1))
    weights = jnp.exp(scores - new_max[:, None])
    new_sum = jnp.sum(weights, axis=1)
    new_acc = jnp.einsum("qkph,kphe->qphe", weights, value_heads)
    attended_time = (new_acc / new_sum[..., None]).reshape(view_maps.shape).astype(jnp.bfloat16)
    refined = (middle.astype(jnp.float32) + project(attended_time, temporal_output)).astype(
        jnp.bfloat16
    )
    return refined


def solution(mesh):
    return jax.shard_map(
        body,
        mesh=mesh,
        in_specs=(P("view", "row", "col", None), P(), P(), P(), P(), P(), P(), P(), P(), P(), P()),
        out_specs=P("view", "row", "col", None),
        check_vma=False,
    )
```

profile of v0, /device:TPU:103, one launch (start us, length us, event | category | flops | bytes accessed | tf_op | source)
XLA Modules:
  0.0 164.0 jit_solution(17304333860771478719)
XLA Ops:
  6.6 1.3 fusion.40
  7.9 1.9 %fusion.28 = bf16[1,4,4,16,768]{4,3,2,1,0:T(8,128)(2,1)S(1)} fusion(bf16[768,768]{1,0:T(8,128)(2,1)} %param.16, bf16[4,4,16,768]{3,2,1,0:T(8,128)(2,1)} %param.13, f32[768]{0:T(1024)} %param.14, f32[4,4,16]{2,1,0:T(4,128)S(1)} %add_rsqrt_fusion.1), kind=kOutput, calls=%fused_computation.46 | convolution fusion | flops 302972928 | bytes 1970176 | tf_op jit(solution)/shard_map/dot_general | solution.py:36
  9.9 0.5 fusion.29
  10.4 1.1 fusion.45
  11.5 4.7 %collective-permute-start = (bf16[2,4,3,16,768]{4,3,2,1,0:T(8,128)(2,1)}, bf16[2,4,3,16,768]{4,3,2,1,0:T(8,128)(2,1)S(1)}, u32[]{:S(2)}, u32[]{:S(2)}) collective-permute-start(bf16[2,4,3,16,768]{4,3,2,1,0:T(8,128)(2,1)} %get-tuple-element.103), channel_id=1, source_target_pairs={{0,8},{8,16},{16,24},{24,32},{32,40},{40,48},{48,56},{1,9},{9,17},... | collective-permute-start | bytes 1769480 | tf_op jit(solution)/shard_map/ppermute | solution.py:20
  16.3 1.9 %collective-permute-start.1 = (bf16[2,4,3,16,768]{4,3,2,1,0:T(8,128)(2,1)}, bf16[2,4,3,16,768]{4,3,2,1,0:T(8,128)(2,1)S(1)}, u32[]{:S(2)}, u32[]{:S(2)}) collective-permute-start(bf16[2,4,3,16,768]{4,3,2,1,0:T(8,128)(2,1)} %get-tuple-element.104), channel_id=1, source_target_pairs={{8,0},{16,8},{24,16},{32,24},{40,32},{48,40},{56,48},{9,1},{17,9},... | collective-permute-start | bytes 1769480 | tf_op jit(solution)/shard_map/ppermute | solution.py:23
  18.2 0.6 reshape.291
  18.9 9.6 %collective-permute-done = bf16[2,4,3,16,768]{4,3,2,1,0:T(8,128)(2,1)S(1)} collective-permute-done((bf16[2,4,3,16,768]{4,3,2,1,0:T(8,128)(2,1)}, bf16[2,4,3,16,768]{4,3,2,1,0:T(8,128)(2,1)S(1)}, u32[]{:S(2)}, u32[]{:S(2)}) %collective-permute-start) | collective-permute-done | bytes 589856 | tf_op jit(solution)/shard_map/ppermute | solution.py:20
  28.6 4.9 %collective-permute-done.1 = bf16[2,4,3,16,768]{4,3,2,1,0:T(8,128)(2,1)S(1)} collective-permute-done((bf16[2,4,3,16,768]{4,3,2,1,0:T(8,128)(2,1)}, bf16[2,4,3,16,768]{4,3,2,1,0:T(8,128)(2,1)S(1)}, u32[]{:S(2)}, u32[]{:S(2)}) %collective-permute-start.1) | collective-permute-done | bytes 589856 | tf_op jit(solution)/shard_map/ppermute | solution.py:23
  33.5 1.3 pad_maximum_fusion.5
  34.8 3.1 %collective-permute-start.2 = (bf16[2,4,10,3,768]{4,3,2,1,0:T(4,128)(2,1)}, bf16[2,4,10,3,768]{4,3,2,1,0:T(4,128)(2,1)}, u32[]{:S(2)}, u32[]{:S(2)}) collective-permute-start(bf16[2,4,10,3,768]{4,3,2,1,0:T(4,128)(2,1)} %get-tuple-element.101), channel_id=1, source_target_pairs={{0,1},{1,2},{2,3},{3,4},{4,5},{5,6},{6,7},{8,9},{9,10},{10,11},{11... | collective-permute-start | bytes 1105928 | tf_op jit(solution)/shard_map/ppermute | solution.py:20
  38.0 2.2 %collective-permute-start.3 = (bf16[2,4,10,3,768]{4,3,2,1,0:T(4,128)(2,1)}, bf16[2,4,10,3,768]{4,3,2,1,0:T(4,128)(2,1)}, u32[]{:S(2)}, u32[]{:S(2)}) collective-permute-start(bf16[2,4,10,3,768]{4,3,2,1,0:T(4,128)(2,1)} %get-tuple-element.102), channel_id=1, source_target_pairs={{1,0},{2,1},{3,2},{4,3},{5,4},{6,5},{7,6},{9,8},{10,9},{11,10},{12... | collective-permute-start | bytes 1105928 | tf_op jit(solution)/shard_map/ppermute | solution.py:23
  40.3 0.6 broadcast_in_dim.38
  40.9 0.7 sub.85
  41.6 2.6 %convolution_convert_fusion.4 = bf16[4,4,16,768]{3,2,1,0:T(8,128)(2,1)} fusion(bf16[768,768]{1,0:T(8,128)(2,1)} %param.15, bf16[4,4,16,768]{3,2,1,0:T(8,128)(2,1)S(1)} %copy-done.2, f32[768]{0:T(1024)} %param.14, f32[4,4,16]{2,1,0:T(4,128)} %copy-done.4), kind=kOutput, calls=%fused_computation.43 | convolution fusion | flops 302972928 | bytes 1970176 | tf_op jit(solution)/shard_map/dot_general | solution.py:36
  44.2 3.8 %collective-permute-done.2 = bf16[2,4,10,3,768]{4,3,2,1,0:T(4,128)(2,1)} collective-permute-done((bf16[2,4,10,3,768]{4,3,2,1,0:T(4,128)(2,1)}, bf16[2,4,10,3,768]{4,3,2,1,0:T(4,128)(2,1)}, u32[]{:S(2)}, u32[]{:S(2)}) %collective-permute-start.2) | collective-permute-done | bytes 368672 | tf_op jit(solution)/shard_map/ppermute | solution.py:20
  48.0 5.0 %collective-permute-done.3 = bf16[2,4,10,3,768]{4,3,2,1,0:T(4,128)(2,1)} collective-permute-done((bf16[2,4,10,3,768]{4,3,2,1,0:T(4,128)(2,1)}, bf16[2,4,10,3,768]{4,3,2,1,0:T(4,128)(2,1)}, u32[]{:S(2)}, u32[]{:S(2)}) %collective-permute-start.3) | collective-permute-done | bytes 368672 | tf_op jit(solution)/shard_map/ppermute | solution.py:23
  53.0 3.1 %pad_maximum_fusion = bf16[2,4,10,22,768]{4,3,2,1,0:T(8,128)(2,1)S(1)} fusion(bf16[2,4,10,3,768]{4,3,2,1,0:T(4,128)(2,1)} %collective-permute-done.3, bf16[2,4,3,16,768]{4,3,2,1,0:T(8,128)(2,1)S(1)} %collective-permute-done.1, bf16[1,4,4,16,768]{4,3,2,1,0:T(8,128)(2,1)S(1)} %fusion.29, bf16[1,4,4,16,768]{4,3,2,1,0:T(8,128)(2,1)S(1)} %fusion.28, ...), kind=kLoop, calls=%fused_computation.26 | loop fusion | flops 16220160 | bytes 5406720 | tf_op jit(solution)/shard_map/concatenate | solution.py:24
  56.1 1.8 %slice_bitcast_fusion = (bf16[4,10,22,768]{3,2,1,0:T(8,128)(2,1)}, bf16[4,10,22,768]{3,2,1,0:T(8,128)(2,1)}) fusion(bf16[2,4,10,22,768]{4,3,2,1,0:T(8,128)(2,1)S(1)} %pad_maximum_fusion), kind=kLoop, calls=%fused_computation.33 | loop fusion | bytes 5406720 | tf_op jit(solution)/shard_map/squeeze | solution.py:115
  57.9 26.6 %while.11 = (s32[]{:T(128)}, bf16[4,4,16,768]{3,2,1,0:T(8,128)(2,1)}, bf16[4,10,22,768]{3,2,1,0:T(8,128)(2,1)}, bf16[4,4,16,768]{3,2,1,0:T(8,128)(2,1)}, bf16[4,...) while((s32[]{:T(128)}, ...), condition=%wide.region_4.5_spmd.clone, body=%wide.region_1.4_spmd.clone.sunk | while | flops 152731136 | bytes 6633009 | solution.py:88
  57.9 1.1 constant_dynamic-slice_fusion.5
  59.0 0.5 reshape.306
  59.7 0.9 constant_dynamic-slice_fusion.6
  60.8 0.6 fusion.71
  61.4 0.3 fusion.72
  61.8 0.5 reshape.308
  62.3 1.1 fusion.73
  63.9 0.7 constant_dynamic-update-slice_fusion.2
  64.5 1.1 constant_dynamic-slice_fusion.5
  65.7 0.5 reshape.306
  66.3 0.9 constant_dynamic-slice_fusion.6
  67.4 0.6 fusion.71
  68.4 0.5 reshape.308
  69.0 1.2 fusion.73
  70.5 0.7 constant_dynamic-update-slice_fusion.2
  71.2 1.1 constant_dynamic-slice_fusion.5
  72.4 0.5 reshape.306
  73.0 0.9 constant_dynamic-slice_fusion.6
  74.1 0.6 fusion.71
  75.1 0.5 reshape.308
  75.6 1.2 fusion.73
  77.2 0.7 constant_dynamic-update-slice_fusion.2
  77.9 1.1 constant_dynamic-slice_fusion.5
  79.0 0.5 reshape.306
  79.7 0.9 constant_dynamic-slice_fusion.6
  80.8 0.6 fusion.71
  81.7 0.5 reshape.308
  82.3 1.2 fusion.73
  83.9 0.7 constant_dynamic-update-slice_fusion.2
  84.5 1.8 %multiply_reduce_fusion = (f32[4,4,16]{2,1,0:T(4,128)S(1)}, f32[4,4,16,768]{3,2,1,0:T(8,128)S(1)}) fusion(bf16[4,4,16,768]{3,2,1,0:T(8,128)(2,1)} %get-tuple-element.37, bf16[768,768]{1,0:T(8,128)(2,1)S(1)} %copy-done, bf16[4,4,16,768]{3,2,1,0:T(8,128)(2,1)} %param.13), kind=kOutput, calls=%fused_computation.67 | convolution fusion | flops 303169280 | bytes 2753536 | tf_op jit(solution)/shard_map/dot_general | solution.py:36
  86.5 1.2 convolution_convert_fusion.2
  88.0 1.2 convolution_convert_fusion.3
  89.2 1.7 %convolution_convert_fusion.1 = bf16[4,4,16,768]{3,2,1,0:T(8,128)(2,1)S(1)} fusion(bf16[4,4,16,768]{3,2,1,0:T(8,128)(2,1)S(1)} %multiply_convert_fusion, bf16[768,768]{1,0:T(8,128)(2,1)} %param.20), kind=kOutput, calls=%fused_computation.40 | convolution fusion | flops 302186496 | bytes 1966080 | tf_op jit(solution)/shard_map/dot_general | solution.py:36
  91.0 0.6 reshape.290
  91.6 23.9 %all-gather.5.cloned.1.call-done = bf16[16,4,16,768]{3,2,1,0:T(8,128)(2,1)} async-done(((bf16[4,4,16,768]{3,2,1,0:T(8,128)(2,1)}), bf16[16,4,16,768]{3,2,1,0:T(8,128)(2,1)}) %all-gather.5.cloned.1.call-update) | async-done | bytes 1572880 | tf_op jit(solution)/shard_map/all_gather | solution.py:131
  115.5 5.9 %reshape.289 = bf16[16,64,12,64]{3,2,1,0:T(8,128)(2,1)} reshape(bf16[16,4,16,768]{3,2,1,0:T(8,128)(2,1)} %all-gather.5.cloned.1.call-done) | data formatting | bytes 3145728 | tf_op jit(solution)/shard_map/reshape | solution.py:131
  121.4 5.0 %bitcast_reduce_fusion = (f32[4,64,12]{0,2,1:T(8,128)S(1)}, f32[64,12,16,4]{2,3,1,0:T(4,128)S(1)}) fusion(bf16[4,64,12,64]{3,2,1,0:T(8,128)(2,1)S(1)} %reshape.290, bf16[16,64,12,64]{3,2,1,0:T(8,128)(2,1)} %reshape.289), kind=kOutput, calls=%fused_computation.29 | convolution fusion | flops 6386688 | bytes 2174976 | tf_op jit(solution)/shard_map/qphe,kphe->qkph/dot_general | solution.py:140
  126.4 1.1 copy-done.1
  127.6 1.9 %fusion.30 = f32[4,64,12]{0,2,1:T(8,128)S(1)} fusion(f32[64,12,16,4]{2,3,1,0:T(4,128)S(1)} %get-tuple-element.108, f32[4,64,12]{0,2,1:T(8,128)S(1)} %broadcast_maximum_fusion), kind=kLoop, calls=%fused_computation.48 | loop fusion | flops 95232 | bytes 221184 | tf_op jit(solution)/shard_map/reduce_sum | solution.py:145
  129.5 13.6 %all-gather.3.cloned.1.call-done = bf16[16,4,16,768]{3,2,1,0:T(8,128)(2,1)} async-done(((bf16[4,4,16,768]{3,2,1,0:T(8,128)(2,1)}), bf16[16,4,16,768]{3,2,1,0:T(8,128)(2,1)}) %all-gather.3.cloned.1.call-update) | async-done | bytes 1572880 | tf_op jit(solution)/shard_map/all_gather | solution.py:135
  143.1 5.9 %reshape.288 = bf16[16,64,12,64]{3,2,1,0:T(8,128)(2,1)} reshape(bf16[16,4,16,768]{3,2,1,0:T(8,128)(2,1)} %all-gather.3.cloned.1.call-done) | data formatting | bytes 3145728 | tf_op jit(solution)/shard_map/reshape | solution.py:136
  148.9 4.9 %fusion.19 = bf16[4,64,12,64]{3,0,2,1:T(4,128)(2,1)S(1)} fusion(bf16[16,64,12,64]{3,2,1,0:T(8,128)(2,1)} %reshape.288, f32[64,12,16,4]{2,3,1,0:T(4,128)} %copy-done.1, f32[4,64,12]{0,2,1:T(8,128)S(1)} %fusion.30, f32[4,64,12]{0,2,1:T(8,128)S(1)} %broadcast_maximum_fusion), kind=kOutput, calls=%fused_computation.31 | convolution fusion | flops 6733824 | bytes 2187264 | tf_op jit(solution)/shard_map/qkph,kphe->qphe/dot_general | solution.py:146
  154.0 0.6 convert_element_type.76
  154.6 2.5 %fusion.27 = bf16[4,4,16,768]{3,2,1,0:T(8,128)(2,1)} fusion(f32[4,4,16,768]{3,2,1,0:T(8,128)S(1)} %get-tuple-element.106, bf16[4,4,16,768]{3,2,1,0:T(8,128)(2,1)S(1)} %convert_element_type.76, bf16[768,768]{1,0:T(8,128)(2,1)} %param.23), kind=kOutput, calls=%fused_computation.39 | convolution fusion | flops 302383104 | bytes 2752512 | tf_op jit(solution)/shard_map/dot_general | solution.py:36
  (55 shorter events, 4.7 us)
Async XLA Ops:
  6.5 78.0 %copy-start = (bf16[768,768]{1,0:T(8,128)(2,1)S(1)}, bf16[768,768]{1,0:T(8,128)(2,1)}, u32[]{:S(2)}) copy-start(bf16[768,768]{1,0:T(8,128)(2,1)} %param.18) | copy-start | bytes 3538948
  6.5 3.3 %copy-start.2 = (bf16[4,4,16,768]{3,2,1,0:T(8,128)(2,1)S(1)}, bf16[4,4,16,768]{3,2,1,0:T(8,128)(2,1)}, u32[]{:S(2)}) copy-start(bf16[4,4,16,768]{3,2,1,0:T(8,128)(2,1)} %param.13) | copy-start | bytes 1179652
  6.5 3.3 %copy-start.9 = (f32[768]{0:T(1024)S(1)}, f32[768]{0:T(1024)}, u32[]{:S(2)}) copy-start(f32[768]{0:T(1024)} %param.14) | copy-start | bytes 9220
  6.5 109.0 %all-gather.5.cloned.1.call-start = ((), (), s32[]{:S(2)}) async-start(), calls=%async_computation.1 | async-start | bytes 1966080 | tf_op jit(solution)/shard_map/all_gather | solution.py:131
  6.5 3.3 %copy-start.6 = (bf16[768,768]{1,0:T(8,128)(2,1)S(1)}, bf16[768,768]{1,0:T(8,128)(2,1)}, u32[]{:S(2)}) copy-start(bf16[768,768]{1,0:T(8,128)(2,1)} %param.17) | copy-start | bytes 3538948
  7.9 2.5 %copy-start.4 = (f32[4,4,16]{2,1,0:T(4,128)}, f32[4,4,16]{2,1,0:T(4,128)S(1)}, u32[]{:S(2)}) copy-start(f32[4,4,16]{2,1,0:T(4,128)S(1)} %add_rsqrt_fusion.1) | copy-start | bytes 3076
  11.5 17.0 %collective-permute-start = (bf16[2,4,3,16,768]{4,3,2,1,0:T(8,128)(2,1)}, bf16[2,4,3,16,768]{4,3,2,1,0:T(8,128)(2,1)S(1)}, u32[]{:S(2)}, u32[]{:S(2)}) collective-permute-start(bf16[2,4,3,16,768]{4,3,2,1,0:T(8,128)(2,1)} %get-tuple-element.103), channel_id=1, source_target_pairs={{0,8},{8,16},{16,24},{24,32},{32,40},{40,48},{48,56},{1,9},{9,17},... | collective-permute-start | bytes 1769480 | tf_op jit(solution)/shard_map/ppermute | solution.py:20
  16.3 17.2 %collective-permute-start.1 = (bf16[2,4,3,16,768]{4,3,2,1,0:T(8,128)(2,1)}, bf16[2,4,3,16,768]{4,3,2,1,0:T(8,128)(2,1)S(1)}, u32[]{:S(2)}, u32[]{:S(2)}) collective-permute-start(bf16[2,4,3,16,768]{4,3,2,1,0:T(8,128)(2,1)} %get-tuple-element.104), channel_id=1, source_target_pairs={{8,0},{16,8},{24,16},{32,24},{40,32},{48,40},{56,48},{9,1},{17,9},... | collective-permute-start | bytes 1769480 | tf_op jit(solution)/shard_map/ppermute | solution.py:23
  34.8 13.2 %collective-permute-start.2 = (bf16[2,4,10,3,768]{4,3,2,1,0:T(4,128)(2,1)}, bf16[2,4,10,3,768]{4,3,2,1,0:T(4,128)(2,1)}, u32[]{:S(2)}, u32[]{:S(2)}) collective-permute-start(bf16[2,4,10,3,768]{4,3,2,1,0:T(4,128)(2,1)} %get-tuple-element.101), channel_id=1, source_target_pairs={{0,1},{1,2},{2,3},{3,4},{4,5},{5,6},{6,7},{8,9},{9,10},{10,11},{11... | collective-permute-start | bytes 1105928 | tf_op jit(solution)/shard_map/ppermute | solution.py:20
  38.0 15.0 %collective-permute-start.3 = (bf16[2,4,10,3,768]{4,3,2,1,0:T(4,128)(2,1)}, bf16[2,4,10,3,768]{4,3,2,1,0:T(4,128)(2,1)}, u32[]{:S(2)}, u32[]{:S(2)}) collective-permute-start(bf16[2,4,10,3,768]{4,3,2,1,0:T(4,128)(2,1)} %get-tuple-element.102), channel_id=1, source_target_pairs={{1,0},{2,1},{3,2},{4,3},{5,4},{6,5},{7,6},{9,8},{10,9},{11,10},{12... | collective-permute-start | bytes 1105928 | tf_op jit(solution)/shard_map/ppermute | solution.py:23
  56.1 1.8 %copy-start.3 = (pred[220]{0:T(512)(128)(4,1)S(1)}, pred[220]{0:T(512)(128)(4,1)}, u32[]{:S(2)}) copy-start(pred[220]{0:T(512)(128)(4,1)} %reshape.291) | copy-start | bytes 664
  84.5 1.8 %copy-start.5 = (f32[768]{0:T(1024)S(1)}, f32[768]{0:T(1024)}, u32[]{:S(2)}) copy-start(f32[768]{0:T(1024)} %param.19) | copy-start | bytes 9220
  84.5 1.9 %copy-start.7 = (bf16[768,768]{1,0:T(8,128)(2,1)S(1)}, bf16[768,768]{1,0:T(8,128)(2,1)}, u32[]{:S(2)}) copy-start(bf16[768,768]{1,0:T(8,128)(2,1)} %param.21) | copy-start | bytes 3538948
  86.5 1.5 copy-start.8
  87.8 55.3 %all-gather.3.cloned.1.call-start = ((), (), s32[]{:S(2)}) async-start(), calls=%async_computation | async-start | bytes 1966080 | tf_op jit(solution)/shard_map/all_gather | solution.py:135
  126.4 1.2 copy-start.1
Sparse Core Ops, SparseCore 0:
  87.9 27.6 all-gather.4
  117.3 25.6 all-gather.2
where the time goes:
time: 167 us; the launch traced here: 164 us
  waiting for transfers between devices  60.8 us (36%)
  local copies, waits for them, and re-layouts  35.8 us (21%)
  matrix products  30.5 us (18%)
  between operations  13.7 us (8%)
  starting transfers between devices  12.2 us (7%)
  other arithmetic  10.8 us (6%)
    all_gather x1, waiting for transfers between devices, body(): lax.all_gather(key_time, 'view', axis=0, tiled=True)  23.9 us
    all_gather x1, waiting for transfers between devices, body(): lax.all_gather(value_time, 'view', axis=0, tiled=True)  13.6 us
    dot_general x8, matrix products, project(): result = jnp.dot(flat, weight_matrix, preferred_element_type=jnp.float32)  13.5 us
    ppermute x2, waiting for transfers between devices, padded(): lax.ppermute(lax.slice_in_dim(block, block.shape[dim] - width, None, axis...  13.4 us
    ppermute x2, waiting for transfers between devices, padded(): lax.ppermute(lax.slice_in_dim(block, 0, width, axis=dim), axis, backward)  9.9 us
    dynamic_slice x8, local copies, waits for them, and re-layouts, neighbour(): return lax.map(one_view, (queries, keys_wide, values_wide))  8.21 us
    ppermute x2, starting transfers between devices, padded(): lax.ppermute(lax.slice_in_dim(block, block.shape[dim] - width, None, axis...  7.85 us
    reshape x1, local copies, waits for them, and re-layouts, body(): lax.all_gather(key_time, 'view', axis=0, tiled=True)  5.86 us
  transfers between devices with their start and end apart: 6, of which 6 were waited for; matrix products, arithmetic and copies ran while one was open for 13% of the time, Pallas kernels for 0%

commit v1 on v0

v1 whole, which is shorter than its diff:
```python
import functools

import jax
import jax.numpy as jnp
from jax import lax
from jax.experimental import pallas as pl
from jax.experimental.pallas import tpu as pltpu
from jax.sharding import PartitionSpec as P

HEADS = 12
HEAD_DIM = 64
RADIUS = 3
D = 768
GROUP = 4
LANES = GROUP * HEAD_DIM
GROUPS = HEADS // GROUP
ROWS = 4
COLS = 16
TOKENS = ROWS * COLS
SLAB = RADIUS * COLS
SIDE = 32
KEYS = TOKENS + 2 * SLAB + 2 * SIDE
VIEWS = 4
ALL_VIEWS = 16
MAP_H = 32
MAP_W = 128

epsilon = 1e-06
very_negative = -1e30
BF = jnp.bfloat16
F32 = jnp.float32
MIB = 1 << 20


def call(body, outs, flops, nbytes, scratch=(), smem_first=False, n_in=0, limit=20, name=None):
    vmem = pl.BlockSpec(memory_space=pltpu.VMEM)
    in_specs = [vmem] * n_in
    if smem_first:
        in_specs[0] = pl.BlockSpec(memory_space=pltpu.SMEM)
    return pl.pallas_call(
        body,
        out_shape=tuple(jax.ShapeDtypeStruct(s, BF) for s in outs),
        in_specs=in_specs,
        out_specs=tuple(vmem for _ in outs),
        scratch_shapes=list(scratch),
        compiler_params=pltpu.CompilerParams(vmem_limit_bytes=limit * MIB),
        cost_estimate=pl.CostEstimate(flops=flops, bytes_accessed=nbytes, transcendentals=0),
        name=name,
    )


def normed(tokens, gain):
    values = tokens.astype(F32)
    mean = jnp.mean(values * values, axis=-1, keepdims=True)
    return (values * lax.rsqrt(mean + epsilon) * gain).astype(BF)


def dot(a, b):
    return jnp.dot(a, b, preferred_element_type=F32)


def own_body(x, gain, wq, wk, wv, q, k, v):
    n = normed(x[...], gain[...])
    q[...] = dot(n, wq[...]).astype(BF)
    k[...] = dot(n, wk[...]).astype(BF)
    v[...] = dot(n, wv[...]).astype(BF)


def sides_body(x, up, down, to_left, to_right):
    i = lax.broadcasted_iota(jnp.int32, (2 * SIDE, TOKENS + 2 * SLAB), 0)
    j = lax.broadcasted_iota(jnp.int32, (2 * SIDE, TOKENS + 2 * SLAB), 1)
    place = RADIUS * (j >> 4) + (j & 15)
    first = ((j & 15) < RADIUS) & (i == place)
    last = ((j & 15) >= COLS - RADIUS) & (i - SIDE == place - (COLS - RADIUS))
    pick = jnp.where(first | last, 1.0, 0.0).astype(BF)
    for view in range(VIEWS):
        wide = jnp.concatenate([up[view], x[view], down[view]], axis=0)
        taken = dot(pick, wide).astype(BF)
        to_left[view] = taken[:SIDE]
        to_right[view] = taken[SIDE:]


def slabs_body(up, down, gain, wk, wv, ku, vu, kd, vd):
    for source, k, v in ((up, ku, vu), (down, kd, vd)):
        n = normed(source[...], gain[...])
        k[...] = dot(n, wk[...]).astype(BF)
        v[...] = dot(n, wv[...]).astype(BF)


def attend(q, keys, values, allowed, spread):
    stacked = jnp.concatenate([q] * GROUP, axis=0)
    stacked = jnp.where(spread, stacked, jnp.zeros_like(stacked))
    scores = lax.dot_general(stacked, keys, (((1,), (1,)), ((), ())), preferred_element_type=F32)
    scores = jnp.where(allowed, scores, very_negative)
    highest = jnp.max(scores, axis=-1, keepdims=True)
    weights = jnp.exp(scores - highest)
    total = jnp.sum(weights, axis=-1, keepdims=True)
    mixed = dot(weights.astype(BF), values) / total
    mixed = jnp.where(spread, mixed, 0.0)
    count = q.shape[0]
    result = mixed[:count]
    for head in range(1, GROUP):
        result = result + mixed[head * count:(head + 1) * count]
    return result.astype(BF)


def spread_mask(count):
    shape = (GROUP * count, LANES)
    row = lax.broadcasted_iota(jnp.int32, shape, 0)
    lane = lax.broadcasted_iota(jnp.int32, shape, 1)
    return (row // count) == (lane // HEAD_DIM)


def window_mask(first_row, first_col):
    shape = (GROUP * TOKENS, KEYS)
    i = lax.broadcasted_iota(jnp.int32, shape, 0) & (TOKENS - 1)
    query_row, query_col = i >> 4, i & 15
    j = lax.broadcasted_iota(jnp.int32, shape, 1)
    up, down, left, right = TOKENS, TOKENS + SLAB, TOKENS + 2 * SLAB, TOKENS + 2 * SLAB + SIDE
    row = jnp.where(j < up, j >> 4, jnp.where(j < down, ((j - up) >> 4) - RADIUS, ((j - down) >> 4) + ROWS))
    col = j & 15
    t = (j - left) & (SIDE - 1)
    t_row = (t * 43) >> 7
    t_col = t - 3 * t_row
    side = j >= left
    row = jnp.where(side, t_row - RADIUS, row)
    col = jnp.where(side, jnp.where(j >= right, t_col + COLS, t_col - RADIUS), col)
    real = jnp.logical_not(side) | (t < RADIUS * (ROWS + 2 * RADIUS))
    near = (jnp.abs(row - query_row) <= RADIUS) & (jnp.abs(col - query_col) <= RADIUS)
    there_row, there_col = first_row + row, first_col + col
    inside = (there_row >= 0) & (there_row < MAP_H) & (there_col >= 0) & (there_col < MAP_W)
    return real & near & inside


def window_body(place, x, q, k, v, ku, vu, kd, vd, left, right, gain, wk, wv, wo, middle, side_k, side_v, out):
    sides = normed(jnp.concatenate([left[...], right[...]], axis=0), gain[...])
    side_k[...] = dot(sides, wk[...]).astype(BF)
    side_v[...] = dot(sides, wv[...]).astype(BF)
    allowed = window_mask(place[0], place[1])
    spread = spread_mask(TOKENS)
    half = VIEWS * SIDE
    for view in range(VIEWS):
        t = slice(view * TOKENS, (view + 1) * TOKENS)
        s = slice(view * SLAB, (view + 1) * SLAB)
        lo = slice(view * SIDE, (view + 1) * SIDE)
        hi = slice(half + view * SIDE, half + (view + 1) * SIDE)
        for group in range(GROUPS):
            f = slice(group * LANES, (group + 1) * LANES)
            keys = jnp.concatenate([k[t, f], ku[s, f], kd[s, f], side_k[lo, f], side_k[hi, f]], axis=0)
            values = jnp.concatenate([v[t, f], vu[s, f], vd[s, f], side_v[lo, f], side_v[hi, f]], axis=0)
            out[t, f] = attend(q[t, f] * 0.125, keys, values, allowed, spread)
    middle[...] = (x[...].astype(F32) + dot(out[...], wo[...])).astype(BF)


def near_body(m, partner, gain, wq, wk, wv, q, k, v, kp, vp):
    own_body(m, gain, wq, wk, wv, q, k, v)
    n = normed(partner[...], gain[...])
    kp[...] = dot(n, wk[...]).astype(BF)
    vp[...] = dot(n, wv[...]).astype(BF)


def views_body(m, q, k, v, kp, vp, far, far_partner, gain, wk, wv, wo, refined, kf, vf, out):
    n = normed(jnp.concatenate([far[...], far_partner[...]], axis=0), gain[...])
    kf[...] = dot(n, wk[...]).astype(BF)
    vf[...] = dot(n, wv[...]).astype(BF)
    spread = spread_mask(TOKENS)
    shape = (GROUP * TOKENS, ALL_VIEWS * COLS)
    i = lax.broadcasted_iota(jnp.int32, shape, 0)
    j = lax.broadcasted_iota(jnp.int32, shape, 1)
    allowed = (i & 15) == (j & 15)
    own = VIEWS * TOKENS

    def rows(ref, row, f, base=0):
        return [ref[base + w * TOKENS + row * COLS:base + w * TOKENS + (row + 1) * COLS, f] for w in range(VIEWS)]

    for row in range(ROWS):
        for group in range(GROUPS):
            f = slice(group * LANES, (group + 1) * LANES)
            queries = jnp.concatenate(rows(q, row, f), axis=0)
            keys = jnp.concatenate(rows(k, row, f) + rows(kp, row, f) + rows(kf, row, f) + rows(kf, row, f, own), axis=0)
            values = jnp.concatenate(rows(v, row, f) + rows(vp, row, f) + rows(vf, row, f) + rows(vf, row, f, own), axis=0)
            mixed = attend(queries * 0.125, keys, values, allowed, spread)
            for w in range(VIEWS):
                out[w * TOKENS + row * COLS:w * TOKENS + (row + 1) * COLS, f] = mixed[w * COLS:(w + 1) * COLS]
    refined[...] = (m[...].astype(F32) + dot(out[...], wo[...])).astype(BF)


def body(
    view_maps,
    gain_spatial,
    spatial_query,
    spatial_key,
    spatial_value,
    spatial_output,
    gain_temporal,
    temporal_query,
    temporal_key,
    temporal_value,
    temporal_output,
):
    own = VIEWS * TOKENS
    x = view_maps.reshape(own, D)
    gain_s = gain_spatial.reshape(1, D)
    gain_t = gain_temporal.reshape(1, D)
    place = jnp.stack([lax.axis_index("row") * ROWS, lax.axis_index("col") * COLS]).astype(jnp.int32)
    forward = [(i, i + 1) for i in range(7)]
    backward = [(i + 1, i) for i in range(7)]
    up = lax.ppermute(view_maps[:, ROWS - RADIUS:], "row", forward)
    down = lax.ppermute(view_maps[:, :RADIUS], "row", backward)
    q, k, v = call(own_body, [(own, D)] * 3, 2 * own * D * D * 3, 6 * MIB, n_in=5, name="own")(
        x, gain_s, spatial_query, spatial_key, spatial_value)
    up = up.reshape(VIEWS, SLAB, D)
    down = down.reshape(VIEWS, SLAB, D)
    to_left, to_right = call(sides_body, [(VIEWS, SIDE, D)] * 2, 10**8, 2 * MIB, n_in=3, name="sides")(
        x.reshape(VIEWS, TOKENS, D), up, down)
    left = lax.ppermute(to_right, "col", forward)
    right = lax.ppermute(to_left, "col", backward)
    slab = VIEWS * SLAB
    ku, vu, kd, vd = call(slabs_body, [(slab, D)] * 4, 2 * slab * D * D * 4, 6 * MIB, n_in=5, name="slabs")(
        up.reshape(slab, D), down.reshape(slab, D), gain_s, spatial_key, spatial_value)
    side = VIEWS * SIDE
    (middle,) = call(
        window_body, [(own, D)], 10**9, 8 * MIB, n_in=15, smem_first=True, name="window",
        scratch=[pltpu.VMEM((2 * side, D), BF), pltpu.VMEM((2 * side, D), BF), pltpu.VMEM((own, D), BF)],
    )(place, x, q, k, v, ku, vu, kd, vd, left.reshape(side, D), right.reshape(side, D), gain_s,
      spatial_key, spatial_value, spatial_output)
    far = lax.ppermute(middle, "view", [(i, i ^ 2) for i in range(4)])
    partner = lax.ppermute(middle, "view", [(i, i ^ 1) for i in range(4)])
    q, k, v, kp, vp = call(near_body, [(own, D)] * 5, 2 * own * D * D * 5, 8 * MIB, n_in=6, name="near")(
        middle, partner, gain_t, temporal_query, temporal_key, temporal_value)
    far_partner = lax.ppermute(far, "view", [(i, i ^ 1) for i in range(4)])
    (refined,) = call(
        views_body, [(own, D)], 10**9, 8 * MIB, n_in=12, name="views",
        scratch=[pltpu.VMEM((2 * own, D), BF), pltpu.VMEM((2 * own, D), BF), pltpu.VMEM((own, D), BF)],
    )(middle, q, k, v, kp, vp, far, far_partner, gain_t, temporal_key, temporal_value, temporal_output)
    return refined.reshape(view_maps.shape)


def solution(mesh):
    return jax.shard_map(
        body,
        mesh=mesh,
        in_specs=(P("view", "row", "col", None), P(), P(), P(), P(), P(), P(), P(), P(), P(), P()),
        out_specs=P("view", "row", "col", None),
        check_vma=False,
    )
```

time: 167 us -> 51.2 us (0.31); the launches traced: 164 us -> 50.9 us
  waiting for transfers between devices: 60.8 us -> 11.6 us
  local copies, waits for them, and re-layouts: 35.8 us -> 5.01 us
  matrix products: 30.5 us -> 0 us
  between operations: 13.7 us -> 0.21 us
  Pallas kernels: 0 us -> 11.7 us
  other arithmetic: 10.8 us -> 0.08 us
  starting transfers between devices: 12.2 us -> 22.3 us
    all_gather x2 -> x0, waiting for transfers between devices: 37.5 us -> none  [the longest x1 23.9 us: body(): lax.all_gather(key_time, 'view', axis=0, tiled=True)]
    dot_general x18 -> x0, matrix products: 30.5 us -> none  [the longest x8 13.5 us: project(): result = jnp.dot(flat, weight_matrix, preferred_element_type=jnp.float32)]
    reshape x15 -> x2, local copies, waits for them, and re-layouts: 17.3 us -> 0.01 us  [the longest x1 0.01 us: body(): gain_s = gain_spatial.reshape(1, D)]
    pallas_call x0 -> x6, Pallas kernels: none -> 11.7 us  [the longest x1 3.94 us: body(): call(views_body, [(own, D)], 10 ** 9, 8 * MIB, n_in=12, name='views', scr...]
    ppermute x4 -> x7, waiting for transfers between devices: 23.3 us -> 11.6 us  [the longest x1 5.04 us: body(): right = lax.ppermute(to_left, 'col', backward)]
    ppermute x4 -> x7, starting transfers between devices: 11.9 us -> 22.3 us  [the longest x1 4.76 us: body(): up = lax.ppermute(view_maps[:, ROWS - RADIUS:], 'row', forward)]
    dynamic_slice x8 -> x0, local copies, waits for them, and re-layouts: 8.21 us -> none  [neighbour(): return lax.map(one_view, (queries, keys_wide, values_wide))]
    reduce_sum x6 -> x0, other arithmetic: 4.57 us -> none  [the longest x1 1.9 us: body(): new_sum = jnp.sum(weights, axis=1)]
  transfers between devices with their start and end apart: 6 -> 7, of which waited for: 6 -> 3; matrix products, arithmetic and copies ran while one was open for 13% -> 0% of each run, Pallas kernels for 0% -> 8%
where the time goes in v1:
time: 51.2 us; the launch traced here: 50.9 us
  starting transfers between devices  22.3 us (44%)
  Pallas kernels  11.7 us (23%)
  waiting for transfers between devices  11.6 us (23%)
  local copies, waits for them, and re-layouts  5.01 us (10%)
    ppermute x1, waiting for transfers between devices, body(): right = lax.ppermute(to_left, 'col', backward)  5.04 us
    ppermute x1, starting transfers between devices, body(): up = lax.ppermute(view_maps[:, ROWS - RADIUS:], 'row', forward)  4.76 us
    ppermute x1, starting transfers between devices, body(): far_partner = lax.ppermute(far, 'view', [(i, i ^ 1) for i in range(4)])  4.09 us
    pallas_call x1, Pallas kernels, body(): call(views_body, [(own, D)], 10 ** 9, 8 * MIB, n_in=12, name='views', scr...  3.94 us
    unnamed x26, local copies, waits for them, and re-layouts  3.85 us
    ppermute x1, waiting for transfers between devices, body(): down = lax.ppermute(view_maps[:, :RADIUS], 'row', backward)  3.74 us
    ppermute x1, starting transfers between devices, body(): partner = lax.ppermute(middle, 'view', [(i, i ^ 1) for i in range(4)])  3.52 us
    pallas_call x1, Pallas kernels, body(): call(window_body, [(own, D)], 10 ** 9, 8 * MIB, n_in=15, smem_first=True,...  3.27 us
  transfers between devices with their start and end apart: 7, of which 3 were waited for; matrix products, arithmetic and copies ran while one was open for 0% of the time, Pallas kernels for 8%

profile of v1, /device:TPU:103, one launch (start us, length us, event | category | flops | bytes accessed | tf_op | source)
XLA Modules:
  0.0 50.9 jit_solution(2843461584640355141)
XLA Ops:
  0.0 0.0 copy-start
  0.0 0.0 copy-start.11
  0.0 1.2 %fusion = (bf16[4,3,16,768]{3,2,1,0:T(8,128)(2,1)S(1)}, bf16[4,3,16,768]{3,2,1,0:T(8,128)(2,1)S(1)}) fusion(bf16[4,4,16,768]{3,2,1,0:T(8,128)(2,1)} %param.11), kind=kLoop, calls=%fused_computation.1 | loop fusion | bytes 1179648 | tf_op jit(solution)/shard_map/slice | solution.py:209
  1.2 4.8 %collective-permute-start = (bf16[4,3,16,768]{3,2,1,0:T(8,128)(2,1)S(1)}, bf16[4,3,16,768]{3,2,1,0:T(8,128)(2,1)S(1)}, u32[]{:S(2)}, u32[]{:S(2)}) collective-permute-start(bf16[4,3,16,768]{3,2,1,0:T(8,128)(2,1)S(1)} %get-tuple-element.34), channel_id=1, source_target_pairs={{0,8},{8,16},{16,24},{24,32},{32,40},{40,48},{48,56},{1,9},{9,17},... | collective-permute-start | bytes 884744 | tf_op jit(solution)/shard_map/ppermute | solution.py:208
  5.9 1.9 %collective-permute-start.1 = (bf16[4,3,16,768]{3,2,1,0:T(8,128)(2,1)S(1)}, bf16[4,3,16,768]{3,2,1,0:T(8,128)(2,1)S(1)}, u32[]{:S(2)}, u32[]{:S(2)}) collective-permute-start(bf16[4,3,16,768]{3,2,1,0:T(8,128)(2,1)S(1)} %get-tuple-element.33), channel_id=1, source_target_pairs={{8,0},{16,8},{24,16},{32,24},{40,32},{48,40},{56,48},{9,1},{17,9},... | collective-permute-start | bytes 884744 | tf_op jit(solution)/shard_map/ppermute | solution.py:209
  7.9 0.0 copy-done.11
  7.9 0.0 copy-done
  7.9 0.0 copy-start.1
  7.9 1.3 %copy-done.1 = bf16[768,768]{1,0:T(8,128)(2,1)S(1)} copy-done((bf16[768,768]{1,0:T(8,128)(2,1)S(1)}, bf16[768,768]{1,0:T(8,128)(2,1)}, u32[]{:S(2)}) %copy-start.1) | copy-done | bytes 1179672
  9.2 0.0 copy-start.3
  9.2 1.3 %copy-done.3 = bf16[768,768]{1,0:T(8,128)(2,1)S(1)} copy-done((bf16[768,768]{1,0:T(8,128)(2,1)S(1)}, bf16[768,768]{1,0:T(8,128)(2,1)}, u32[]{:S(2)}) %copy-start.3) | copy-done | bytes 1179672
  10.4 0.0 copy-start.5
  10.4 1.3 %copy-done.5 = bf16[768,768]{1,0:T(8,128)(2,1)S(1)} copy-done((bf16[768,768]{1,0:T(8,128)(2,1)S(1)}, bf16[768,768]{1,0:T(8,128)(2,1)}, u32[]{:S(2)}) %copy-start.5) | copy-done | bytes 1179672
  11.7 0.0 copy-start.2
  11.7 0.0 copy-start.4
  11.7 1.2 %own.1 = (bf16[256,768]{1,0:T(8,128)(2,1)S(1)}, bf16[256,768]{1,0:T(8,128)(2,1)S(1)}, bf16[256,768]{1,0:T(8,128)(2,1)S(1)}) custom-call(bf16[256,768]{1,0:T(8,128)(2,1)S(1)} %bitcast.11, f32[1,768]{1,0:T(1,128)S(1)} %reshape.25.gain, bf16[768,768]{1,0:T(8,128)(2,1)S(1)} %copy-done.5, bf16[768,768]{1,0:T(8,128)(2,1)S(1)} %copy-done.1, ...), custom_call_target="tpu_custom_call" | custom-call | flops 905969664 | bytes 6291456 | tf_op jit(solution)/shard_map/own/pallas_call | solution.py:210
  12.9 0.0 collective-permute-done
  12.9 3.7 %collective-permute-done.1 = bf16[4,3,16,768]{3,2,1,0:T(8,128)(2,1)S(1)} collective-permute-done((bf16[4,3,16,768]{3,2,1,0:T(8,128)(2,1)S(1)}, bf16[4,3,16,768]{3,2,1,0:T(8,128)(2,1)S(1)}, u32[]{:S(2)}, u32[]{:S(2)}) %collective-permute-start.1) | collective-permute-done | bytes 294944 | tf_op jit(solution)/shard_map/ppermute | solution.py:209
  16.6 0.3 sides.1
  16.9 3.1 %collective-permute-start.2 = (bf16[4,32,768]{2,1,0:T(8,128)(2,1)S(1)}, bf16[4,32,768]{2,1,0:T(8,128)(2,1)S(1)}, u32[]{:S(2)}, u32[]{:S(2)}) collective-permute-start(bf16[4,32,768]{2,1,0:T(8,128)(2,1)S(1)} %get-tuple-element.26), channel_id=1, source_target_pairs={{0,1},{1,2},{2,3},{3,4},{4,5},{5,6},{6,7},{8,9},{9,10},{10,11},{11... | collective-permute-start | bytes 589832 | tf_op jit(solution)/shard_map/ppermute | solution.py:216
  20.1 2.2 %collective-permute-start.3 = (bf16[4,32,768]{2,1,0:T(8,128)(2,1)S(1)}, bf16[4,32,768]{2,1,0:T(8,128)(2,1)S(1)}, u32[]{:S(2)}, u32[]{:S(2)}) collective-permute-start(bf16[4,32,768]{2,1,0:T(8,128)(2,1)S(1)} %get-tuple-element.27), channel_id=1, source_target_pairs={{1,0},{2,1},{3,2},{4,3},{5,4},{6,5},{7,6},{9,8},{10,9},{11,10},{12... | collective-permute-start | bytes 589832 | tf_op jit(solution)/shard_map/ppermute | solution.py:217
  22.2 0.1 pad_add_fusion.place
  22.3 0.0 copy-done.2
  22.3 0.0 copy-done.4
  22.3 0.0 copy-start.6
  22.3 1.2 %slabs.1 = (bf16[192,768]{1,0:T(8,128)(2,1)S(1)}, bf16[192,768]{1,0:T(8,128)(2,1)S(1)}, bf16[192,768]{1,0:T(8,128)(2,1)S(1)}, bf16[192,768]{1,0:T(8,128)(2,1)S(1)}) custom-call(bf16[192,768]{1,0:T(8,128)(2,1)S(1)} %bitcast.15, bf16[192,768]{1,0:T(8,128)(2,1)S(1)} %bitcast.17, f32[1,768]{1,0:T(1,128)S(1)} %reshape.25.gain, bf16[768,768]{1,0:T(8,128)(2,1)S(1)} %copy-done.2, ...), custom_call_target="tpu_custom_call" | custom-call | flops 905969664 | bytes 6291456 | tf_op jit(solution)/shard_map/slabs/pallas_call | solution.py:219
  23.5 0.0 collective-permute-done.2
  23.6 5.0 %collective-permute-done.3 = bf16[4,32,768]{2,1,0:T(8,128)(2,1)S(1)} collective-permute-done((bf16[4,32,768]{2,1,0:T(8,128)(2,1)S(1)}, bf16[4,32,768]{2,1,0:T(8,128)(2,1)S(1)}, u32[]{:S(2)}, u32[]{:S(2)}) %collective-permute-start.3) | collective-permute-done | bytes 196640 | tf_op jit(solution)/shard_map/ppermute | solution.py:217
  28.6 0.0 copy-done.6
  28.6 0.0 copy-start.12
  28.6 0.0 copy-start.7
  28.6 0.0 copy-start.8
  28.6 0.0 copy-start.10
  28.6 3.3 %window.1.m = bf16[256,768]{1,0:T(8,128)(2,1)S(1)} custom-call(s32[2]{0:T(128)S(1)} %pad_add_fusion.place, bf16[256,768]{1,0:T(8,128)(2,1)S(1)} %bitcast.13, bf16[256,768]{1,0:T(8,128)(2,1)S(1)} %get-tuple-element.19.q, bf16[256,768]{1,0:T(8,128)(2,1)S(1)} %get-tuple-element.20.k, bf16[256,768]{1,0:T(8,128)(2,1)S(1)} %get-tuple-element.21.v, ...), custom_call_target="tpu_custom_call" | custom-call | flops 1000000000 | bytes 8388608 | tf_op jit(solution)/shard_map/window/pallas_call | solution.py:222
  31.9 2.7 %collective-permute-start.5 = (bf16[256,768]{1,0:T(8,128)(2,1)S(1)}, bf16[256,768]{1,0:T(8,128)(2,1)S(1)}, u32[]{:S(2)}, u32[]{:S(2)}) collective-permute-start(bf16[256,768]{1,0:T(8,128)(2,1)S(1)} %window.1.m), channel_id=1, source_target_pairs={{0,128},{64,192},{128,0},{192,64},{1,129},{65,193},{129,1},{193,65... | collective-permute-start | bytes 1179656 | tf_op jit(solution)/shard_map/ppermute | solution.py:227
  34.6 3.5 %collective-permute-start.4 = (bf16[256,768]{1,0:T(8,128)(2,1)S(1)}, bf16[256,768]{1,0:T(8,128)(2,1)S(1)}, u32[]{:S(2)}, u32[]{:S(2)}) collective-permute-start(bf16[256,768]{1,0:T(8,128)(2,1)S(1)} %window.1.m), channel_id=1, source_target_pairs={{0,64},{64,0},{128,192},{192,128},{1,65},{65,1},{129,193},{193,129... | collective-permute-start | bytes 1179656 | tf_op jit(solution)/shard_map/ppermute | solution.py:228
  38.1 2.8 %collective-permute-done.5.far = bf16[256,768]{1,0:T(8,128)(2,1)S(1)} collective-permute-done((bf16[256,768]{1,0:T(8,128)(2,1)S(1)}, bf16[256,768]{1,0:T(8,128)(2,1)S(1)}, u32[]{:S(2)}, u32[]{:S(2)}) %collective-permute-start.5) | collective-permute-done | bytes 393248 | tf_op jit(solution)/shard_map/ppermute | solution.py:227
  40.9 4.1 %collective-permute-start.6 = (bf16[256,768]{1,0:T(8,128)(2,1)S(1)}, bf16[256,768]{1,0:T(8,128)(2,1)S(1)}, u32[]{:S(2)}, u32[]{:S(2)}) collective-permute-start(bf16[256,768]{1,0:T(8,128)(2,1)S(1)} %collective-permute-done.5.far), channel_id=1, source_target_pairs={{0,64},{64,0},{128,192},{192,128},{1,65},{65,1},{129,193},{193,129... | collective-permute-start | bytes 1179656 | tf_op jit(solution)/shard_map/ppermute | solution.py:231
  45.0 0.0 copy-done.12
  45.0 0.0 copy-start.9
  45.0 0.0 collective-permute-done.4.partner
  45.0 0.0 copy-done.7
  45.1 0.0 copy-done.8
  45.1 0.0 copy-done.10
  45.1 1.8 %near.1 = (bf16[256,768]{1,0:T(8,128)(2,1)S(1)}, bf16[256,768]{1,0:T(8,128)(2,1)S(1)}, bf16[256,768]{1,0:T(8,128)(2,1)S(1)}, bf16[256,768]{1,0:T(8,128)(2,1)S(1)}, bf16[256,768]{1,0:T(8,128)(2,1)S(1)}) custom-call(bf16[256,768]{1,0:T(8,128)(2,1)S(1)} %window.1.m, bf16[256,768]{1,0:T(8,128)(2,1)S(1)} %collective-permute-done.4.partner, ...), custom_call_target="tpu_custom_call" | custom-call | flops 1509949440 | bytes 8388608 | tf_op jit(solution)/shard_map/near/pallas_call | solution.py:229
  46.9 0.0 collective-permute-done.6.far_partner
  46.9 0.0 copy-done.9
  46.9 3.9 %views.1 = bf16[256,768]{1,0:T(8,128)(2,1)} custom-call(bf16[256,768]{1,0:T(8,128)(2,1)S(1)} %window.1.m, bf16[256,768]{1,0:T(8,128)(2,1)S(1)} %get-tuple-element.28.q, bf16[256,768]{1,0:T(8,128)(2,1)S(1)} %get-tuple-element.29.k, bf16[256,768]{1,0:T(8,128)(2,1)S(1)} %get-tuple-element.30.v, bf16[256,768]{1,0:T(8,128)(2,1)S(1)} %get-tuple-element.31.kp, ...), custom_call_target="tpu_custom_call" | custom-call | flops 1000000000 | bytes 8388608 | tf_op jit(solution)/shard_map/views/pallas_call | solution.py:232
  (2 shorter events, 0.0 us)
Async XLA Ops:
  0.0 7.9 %copy-start = (bf16[4,4,16,768]{3,2,1,0:T(8,128)(2,1)S(1)}, bf16[4,4,16,768]{3,2,1,0:T(8,128)(2,1)}, u32[]{:S(2)}) copy-start(bf16[4,4,16,768]{3,2,1,0:T(8,128)(2,1)} %param.11) | copy-start | bytes 1179652
  0.0 7.9 %copy-start.11 = (f32[768]{0:T(1024)S(1)}, f32[768]{0:T(1024)}, u32[]{:S(2)}) copy-start(f32[768]{0:T(1024)} %param.12) | copy-start | bytes 9220
  1.2 11.7 %collective-permute-start = (bf16[4,3,16,768]{3,2,1,0:T(8,128)(2,1)S(1)}, bf16[4,3,16,768]{3,2,1,0:T(8,128)(2,1)S(1)}, u32[]{:S(2)}, u32[]{:S(2)}) collective-permute-start(bf16[4,3,16,768]{3,2,1,0:T(8,128)(2,1)S(1)} %get-tuple-element.34), channel_id=1, source_target_pairs={{0,8},{8,16},{16,24},{24,32},{32,40},{40,48},{48,56},{1,9},{9,17},... | collective-permute-start | bytes 884744 | tf_op jit(solution)/shard_map/ppermute | solution.py:208
  5.9 10.7 %collective-permute-start.1 = (bf16[4,3,16,768]{3,2,1,0:T(8,128)(2,1)S(1)}, bf16[4,3,16,768]{3,2,1,0:T(8,128)(2,1)S(1)}, u32[]{:S(2)}, u32[]{:S(2)}) collective-permute-start(bf16[4,3,16,768]{3,2,1,0:T(8,128)(2,1)S(1)} %get-tuple-element.33), channel_id=1, source_target_pairs={{8,0},{16,8},{24,16},{32,24},{40,32},{48,40},{56,48},{9,1},{17,9},... | collective-permute-start | bytes 884744 | tf_op jit(solution)/shard_map/ppermute | solution.py:209
  7.9 1.3 %copy-start.1 = (bf16[768,768]{1,0:T(8,128)(2,1)S(1)}, bf16[768,768]{1,0:T(8,128)(2,1)}, u32[]{:S(2)}) copy-start(bf16[768,768]{1,0:T(8,128)(2,1)} %wk.7) | copy-start | bytes 3538948
  9.2 1.3 %copy-start.3 = (bf16[768,768]{1,0:T(8,128)(2,1)S(1)}, bf16[768,768]{1,0:T(8,128)(2,1)}, u32[]{:S(2)}) copy-start(bf16[768,768]{1,0:T(8,128)(2,1)} %wv.7) | copy-start | bytes 3538948
  10.4 1.3 %copy-start.5 = (bf16[768,768]{1,0:T(8,128)(2,1)S(1)}, bf16[768,768]{1,0:T(8,128)(2,1)}, u32[]{:S(2)}) copy-start(bf16[768,768]{1,0:T(8,128)(2,1)} %wq.2) | copy-start | bytes 3538948
  11.7 10.6 %copy-start.2 = (bf16[768,768]{1,0:T(8,128)(2,1)S(1)}, bf16[768,768]{1,0:T(8,128)(2,1)}, u32[]{:S(2)}) copy-start(bf16[768,768]{1,0:T(8,128)(2,1)} %wk.7) | copy-start | bytes 3538948
  11.7 10.6 %copy-start.4 = (bf16[768,768]{1,0:T(8,128)(2,1)S(1)}, bf16[768,768]{1,0:T(8,128)(2,1)}, u32[]{:S(2)}) copy-start(bf16[768,768]{1,0:T(8,128)(2,1)} %wv.7) | copy-start | bytes 3538948
  16.9 6.6 %collective-permute-start.2 = (bf16[4,32,768]{2,1,0:T(8,128)(2,1)S(1)}, bf16[4,32,768]{2,1,0:T(8,128)(2,1)S(1)}, u32[]{:S(2)}, u32[]{:S(2)}) collective-permute-start(bf16[4,32,768]{2,1,0:T(8,128)(2,1)S(1)} %get-tuple-element.26), channel_id=1, source_target_pairs={{0,1},{1,2},{2,3},{3,4},{4,5},{5,6},{6,7},{8,9},{9,10},{10,11},{11... | collective-permute-start | bytes 589832 | tf_op jit(solution)/shard_map/ppermute | solution.py:216
  20.1 8.5 %collective-permute-start.3 = (bf16[4,32,768]{2,1,0:T(8,128)(2,1)S(1)}, bf16[4,32,768]{2,1,0:T(8,128)(2,1)S(1)}, u32[]{:S(2)}, u32[]{:S(2)}) collective-permute-start(bf16[4,32,768]{2,1,0:T(8,128)(2,1)S(1)} %get-tuple-element.27), channel_id=1, source_target_pairs={{1,0},{2,1},{3,2},{4,3},{5,4},{6,5},{7,6},{9,8},{10,9},{11,10},{12... | collective-permute-start | bytes 589832 | tf_op jit(solution)/shard_map/ppermute | solution.py:217
  22.3 6.3 %copy-start.6 = (bf16[768,768]{1,0:T(8,128)(2,1)S(1)}, bf16[768,768]{1,0:T(8,128)(2,1)}, u32[]{:S(2)}) copy-start(bf16[768,768]{1,0:T(8,128)(2,1)} %wo.2) | copy-start | bytes 3538948
  28.6 16.4 %copy-start.12 = (f32[768]{0:T(1024)S(1)}, f32[768]{0:T(1024)}, u32[]{:S(2)}) copy-start(f32[768]{0:T(1024)} %param.17) | copy-start | bytes 9220
  28.6 16.4 %copy-start.7 = (bf16[768,768]{1,0:T(8,128)(2,1)S(1)}, bf16[768,768]{1,0:T(8,128)(2,1)}, u32[]{:S(2)}) copy-start(bf16[768,768]{1,0:T(8,128)(2,1)} %wk.9) | copy-start | bytes 3538948
  28.6 16.5 %copy-start.8 = (bf16[768,768]{1,0:T(8,128)(2,1)S(1)}, bf16[768,768]{1,0:T(8,128)(2,1)}, u32[]{:S(2)}) copy-start(bf16[768,768]{1,0:T(8,128)(2,1)} %wv.9) | copy-start | bytes 3538948
  28.6 16.5 %copy-start.10 = (bf16[768,768]{1,0:T(8,128)(2,1)S(1)}, bf16[768,768]{1,0:T(8,128)(2,1)}, u32[]{:S(2)}) copy-start(bf16[768,768]{1,0:T(8,128)(2,1)} %wq.3) | copy-start | bytes 3538948
  31.9 9.0 %collective-permute-start.5 = (bf16[256,768]{1,0:T(8,128)(2,1)S(1)}, bf16[256,768]{1,0:T(8,128)(2,1)S(1)}, u32[]{:S(2)}, u32[]{:S(2)}) collective-permute-start(bf16[256,768]{1,0:T(8,128)(2,1)S(1)} %window.1.m), channel_id=1, source_target_pairs={{0,128},{64,192},{128,0},{192,64},{1,129},{65,193},{129,1},{193,65... | collective-permute-start | bytes 1179656 | tf_op jit(solution)/shard_map/ppermute | solution.py:227
  34.6 10.4 %collective-permute-start.4 = (bf16[256,768]{1,0:T(8,128)(2,1)S(1)}, bf16[256,768]{1,0:T(8,128)(2,1)S(1)}, u32[]{:S(2)}, u32[]{:S(2)}) collective-permute-start(bf16[256,768]{1,0:T(8,128)(2,1)S(1)} %window.1.m), channel_id=1, source_target_pairs={{0,64},{64,0},{128,192},{192,128},{1,65},{65,1},{129,193},{193,129... | collective-permute-start | bytes 1179656 | tf_op jit(solution)/shard_map/ppermute | solution.py:228
  40.9 6.0 %collective-permute-start.6 = (bf16[256,768]{1,0:T(8,128)(2,1)S(1)}, bf16[256,768]{1,0:T(8,128)(2,1)S(1)}, u32[]{:S(2)}, u32[]{:S(2)}) collective-permute-start(bf16[256,768]{1,0:T(8,128)(2,1)S(1)} %collective-permute-done.5.far), channel_id=1, source_target_pairs={{0,64},{64,0},{128,192},{192,128},{1,65},{65,1},{129,193},{193,129... | collective-permute-start | bytes 1179656 | tf_op jit(solution)/shard_map/ppermute | solution.py:231
  45.0 1.9 %copy-start.9 = (bf16[768,768]{1,0:T(8,128)(2,1)S(1)}, bf16[768,768]{1,0:T(8,128)(2,1)}, u32[]{:S(2)}) copy-start(bf16[768,768]{1,0:T(8,128)(2,1)} %wo.3) | copy-start | bytes 3538948

commit v2 on v1

v2 whole, which is shorter than its diff:
```python
import functools

import jax
import jax.numpy as jnp
from jax import lax
from jax.experimental import pallas as pl
from jax.experimental.pallas import tpu as pltpu
from jax.sharding import PartitionSpec as P


HEADS = 12
HEAD_DIM = 64
RADIUS = 3
CHUNKS = 2
D = 768
GROUP = 4
LANES = GROUP * HEAD_DIM
GROUPS = HEADS // GROUP
ROWS = 4
COLS = 16
TOKENS = ROWS * COLS
SLAB = RADIUS * COLS
SIDE = 32
KEYS = TOKENS + 2 * SLAB + 2 * SIDE
VIEWS = 4
PART = VIEWS // CHUNKS
ALL_VIEWS = 16
MAP_H = 32
MAP_W = 128

epsilon = 1e-06
very_negative = -1e30
BF = jnp.bfloat16
F32 = jnp.float32
MIB = 1 << 20


def call(body, outs, flops, nbytes, scratch=(), n_in=0, limit=20):
    vmem = pl.BlockSpec(memory_space=pltpu.VMEM)
    return pl.pallas_call(
        body,
        out_shape=tuple(jax.ShapeDtypeStruct(s, BF) if isinstance(s, tuple) else s for s in outs),
        in_specs=[vmem] * n_in,
        out_specs=tuple(vmem for _ in outs),
        scratch_shapes=list(scratch),
        compiler_params=pltpu.CompilerParams(vmem_limit_bytes=limit * MIB),
        cost_estimate=pl.CostEstimate(flops=flops, bytes_accessed=nbytes, transcendentals=0),
    )


def normed(tokens, gain):
    values = tokens.astype(F32)
    mean = jnp.mean(values * values, axis=-1, keepdims=True)
    return (values * lax.rsqrt(mean + epsilon) * gain).astype(BF)


def dot(a, b):
    return jnp.dot(a, b, preferred_element_type=F32)


def own_body(x, gain, wq, wk, wv, q, k, v):
    n = normed(x[...], gain[...])
    q[...] = dot(n, wq[...]).astype(BF)
    k[...] = dot(n, wk[...]).astype(BF)
    v[...] = dot(n, wv[...]).astype(BF)


def sides_body(x, a, b, to_a, to_b):
    shape = (2 * SIDE, TOKENS + 2 * SLAB)
    i = lax.broadcasted_iota(jnp.int32, shape, 0)
    j = lax.broadcasted_iota(jnp.int32, shape, 1)
    odd = lax.axis_index("col") & 1
    base = jnp.where((i >= SIDE) == (odd == 1), COLS - RADIUS, 0)
    t = i & (SIDE - 1)
    col = (j & 15) - base
    chosen = (col >= 0) & (col < RADIUS) & (t == RADIUS * (j >> 4) + col)
    pick = jnp.where(chosen, 1.0, 0.0).astype(BF)
    for view in range(VIEWS):
        own = view * TOKENS
        wide = jnp.concatenate([a[view], x[own:own + TOKENS], b[view]], axis=0)
        taken = dot(pick, wide).astype(BF)
        to_a[view] = taken[:SIDE]
        to_b[view] = taken[SIDE:]


def slabs_body(a, b, gain, wk, wv, ka, va, kb, vb):
    for source, k, v in ((a, ka, va), (b, kb, vb)):
        n = normed(source[...], gain[...])
        k[...] = dot(n, wk[...]).astype(BF)
        v[...] = dot(n, wv[...]).astype(BF)


def compact(full, spread):
    full = jnp.where(spread, full, 0.0)
    count = full.shape[0] // GROUP
    result = full[:count]
    for head in range(1, GROUP):
        result = result + full[head * count:(head + 1) * count]
    return result


def partial_attend(q, keys, values, allowed, spread):
    stacked = jnp.concatenate([q] * GROUP, axis=0)
    stacked = jnp.where(spread, stacked, jnp.zeros_like(stacked))
    scores = lax.dot_general(stacked, keys, (((1,), (1,)), ((), ())), preferred_element_type=F32)
    scores = jnp.where(allowed, scores, very_negative)
    highest = jnp.max(scores, axis=-1, keepdims=True)
    weights = jnp.exp(scores - highest)
    total = jnp.sum(weights, axis=-1, keepdims=True)
    return dot(weights.astype(BF), values), highest, total


def attend(q, keys, values, allowed, spread):
    mixed, _, total = partial_attend(q, keys, values, allowed, spread)
    return compact(mixed / total, spread).astype(BF)


def spread_mask(count):
    shape = (GROUP * count, LANES)
    row = lax.broadcasted_iota(jnp.int32, shape, 0)
    lane = lax.broadcasted_iota(jnp.int32, shape, 1)
    return (row // count) == (lane // HEAD_DIM)


def window_mask(first_row, first_col):
    flat = (1, KEYS)
    j = lax.broadcasted_iota(jnp.int32, flat, 1)
    odd_row = ((first_row >> 2) & 1) == 1
    odd_col = ((first_col >> 4) & 1) == 1
    base_a = jnp.where(odd_row, -RADIUS, ROWS)
    base_b = jnp.where(odd_row, ROWS, -RADIUS)
    slab_a, slab_b, side_a, side_b = TOKENS, TOKENS + SLAB, TOKENS + 2 * SLAB, TOKENS + 2 * SLAB + SIDE
    row = jnp.where(j < slab_a, j >> 4, jnp.where(j < slab_b, ((j - slab_a) >> 4) + base_a, ((j - slab_b) >> 4) + base_b))
    t = (j - side_a) & (SIDE - 1)
    t_row = (t * 43) >> 7
    t_col = t - RADIUS * t_row
    wide_row = jnp.where(t_row < RADIUS, t_row + base_a, jnp.where(t_row < RADIUS + ROWS, t_row - RADIUS, t_row - RADIUS - ROWS + base_b))
    side = j >= side_a
    row = jnp.where(side, wide_row, row)
    at_right = (j >= side_b) == odd_col
    col = jnp.where(side, jnp.where(at_right, t_col + COLS, t_col - RADIUS), j & 15)
    real = jnp.logical_not(side) | (t < RADIUS * (ROWS + 2 * RADIUS))
    there_row, there_col = first_row + row, first_col + col
    inside = (there_row >= 0) & (there_row < MAP_H) & (there_col >= 0) & (there_col < MAP_W)
    row = jnp.where(real & inside, row, 1000)
    shape = (TOKENS, KEYS)
    i = lax.broadcasted_iota(jnp.int32, shape, 0)
    near = (jnp.abs(row - (i >> 4)) <= RADIUS) & (jnp.abs(col - (i & 15)) <= RADIUS)
    tall = jnp.concatenate([near.astype(jnp.int32)] * GROUP, axis=0)
    return tall > 0


def window_body(chunk, x, q, k, v, ka, va, kb, vb, side_a, side_b, gain, wk, wv, wo, middle, side_k, side_v, out):
    first = chunk * PART
    views = slice(first * SIDE, (first + PART) * SIDE)
    sides = normed(jnp.concatenate([side_a[views], side_b[views]], axis=0), gain[...])
    side_k[...] = dot(sides, wk[...]).astype(BF)
    side_v[...] = dot(sides, wv[...]).astype(BF)
    allowed = window_mask(lax.axis_index("row") * ROWS, lax.axis_index("col") * COLS)
    spread = spread_mask(TOKENS)
    half = PART * SIDE
    for view in range(PART):
        o = slice(view * TOKENS, (view + 1) * TOKENS)
        t = slice((first + view) * TOKENS, (first + view + 1) * TOKENS)
        s = slice((first + view) * SLAB, (first + view + 1) * SLAB)
        lo = slice(view * SIDE, (view + 1) * SIDE)
        hi = slice(half + view * SIDE, half + (view + 1) * SIDE)
        for group in range(GROUPS):
            f = slice(group * LANES, (group + 1) * LANES)
            keys = jnp.concatenate([k[t, f], ka[s, f], kb[s, f], side_k[lo, f], side_k[hi, f]], axis=0)
            values = jnp.concatenate([v[t, f], va[s, f], vb[s, f], side_v[lo, f], side_v[hi, f]], axis=0)
            out[o, f] = attend(q[t, f] * 0.125, keys, values, allowed, spread)
    middle[...] = (x[first * TOKENS:(first + PART) * TOKENS].astype(F32) + dot(out[...], wo[...])).astype(BF)


def same_place(count):
    shape = (GROUP * TOKENS, count)
    i = lax.broadcasted_iota(jnp.int32, shape, 0)
    j = lax.broadcasted_iota(jnp.int32, shape, 1)
    return (i & 15) == (j & 15)


def row_of(refs, row, f):
    return jnp.concatenate(
        [ref[w * TOKENS + row * COLS:w * TOKENS + (row + 1) * COLS, f] for ref in refs for w in range(ref.shape[0] // TOKENS)],
        axis=0,
    )


def near_body(*refs):
    middles, partners = refs[:CHUNKS], refs[CHUNKS:2 * CHUNKS]
    gain, wq, wk, wv, q, mixed, highest, total, k, v, kp, vp = refs[2 * CHUNKS:]
    n = normed(jnp.concatenate([r[...] for r in middles], axis=0), gain[...])
    q[...] = (dot(n, wq[...]).astype(BF) * 0.125).astype(BF)
    k[...] = dot(n, wk[...]).astype(BF)
    v[...] = dot(n, wv[...]).astype(BF)
    n = normed(jnp.concatenate([r[...] for r in partners], axis=0), gain[...])
    kp[...] = dot(n, wk[...]).astype(BF)
    vp[...] = dot(n, wv[...]).astype(BF)
    spread = spread_mask(TOKENS)
    allowed = same_place(ALL_VIEWS // 2 * COLS)
    for row in range(ROWS):
        t = slice(row * TOKENS, (row + 1) * TOKENS)
        for group in range(GROUPS):
            f = slice(group * LANES, (group + 1) * LANES)
            m, h, s = partial_attend(row_of([q], row, f), row_of([k, kp], row, f), row_of([v, vp], row, f), allowed, spread)
            mixed[t, f] = compact(m, spread)
            highest[t, f] = compact(h, spread)
            total[t, f] = compact(s, spread)


def far_body(far, gain, wk, wv, k, v):
    n = normed(far[...], gain[...])
    k[...] = dot(n, wk[...]).astype(BF)
    v[...] = dot(n, wv[...]).astype(BF)


def views_body(*refs):
    middles, (q, mixed, highest, total) = refs[:CHUNKS], refs[CHUNKS:CHUNKS + 4]
    refs = refs[CHUNKS + 4:]
    keys, values = list(refs[:2 * CHUNKS - 1]), list(refs[2 * CHUNKS - 1:4 * CHUNKS - 2])
    last, gain, wk, wv, wo, refined, kl, vl, out = refs[4 * CHUNKS - 2:]
    far_body(last, gain, wk, wv, kl, vl)
    keys.append(kl)
    values.append(vl)
    spread = spread_mask(TOKENS)
    allowed = same_place(ALL_VIEWS // 2 * COLS)
    for row in range(ROWS):
        t = slice(row * TOKENS, (row + 1) * TOKENS)
        for group in range(GROUPS):
            f = slice(group * LANES, (group + 1) * LANES)
            m, h, s = partial_attend(row_of([q], row, f), row_of(keys, row, f), row_of(values, row, f), allowed, spread)
            m, h, s = compact(m, spread), compact(h, spread), compact(s, spread)
            top = jnp.maximum(h, highest[t, f])
            late, early = jnp.exp(h - top), jnp.exp(highest[t, f] - top)
            full = (m * late + mixed[t, f] * early) / (s * late + total[t, f] * early)
            full = full.astype(BF)
            for w in range(VIEWS):
                out[w * TOKENS + row * COLS:w * TOKENS + (row + 1) * COLS, f] = full[w * COLS:(w + 1) * COLS]
    middle = jnp.concatenate([r[...] for r in middles], axis=0)
    refined[...] = (middle.astype(F32) + dot(out[...], wo[...])).astype(BF)


def swap(value, axis, first):
    count = lax.axis_size(axis)
    pairs = [(i, i + 1) for i in range(first, count - 1, 2)]
    return lax.ppermute(value, axis, pairs + [(j, i) for i, j in pairs])


def across(value, step):
    return lax.ppermute(value, "view", [(i, i ^ step) for i in range(4)])


def body(
    view_maps,
    gain_spatial,
    spatial_query,
    spatial_key,
    spatial_value,
    spatial_output,
    gain_temporal,
    temporal_query,
    temporal_key,
    temporal_value,
    temporal_output,
):
    own = VIEWS * TOKENS
    part = PART * TOKENS
    x = view_maps.reshape(own, D)
    gain_s = gain_spatial.reshape(1, D)
    gain_t = gain_temporal.reshape(1, D)
    odd = lax.axis_index("row") & 1
    a = swap(lax.dynamic_slice_in_dim(view_maps, 1 - odd, RADIUS, axis=1), "row", 0)
    b = swap(lax.dynamic_slice_in_dim(view_maps, odd, RADIUS, axis=1), "row", 1)
    q, k, v = call(own_body, [(own, D)] * 3, 2 * own * D * D * 3, 6 * MIB, n_in=5)(
        x, gain_s, spatial_query, spatial_key, spatial_value)
    slab, side = VIEWS * SLAB, VIEWS * SIDE
    to_a, to_b = call(sides_body, [(VIEWS, SIDE, D)] * 2, 10**8, 2 * MIB, n_in=3)(
        x, a.reshape(VIEWS, SLAB, D), b.reshape(VIEWS, SLAB, D))
    side_a = swap(to_a, "col", 0).reshape(side, D)
    side_b = swap(to_b, "col", 1).reshape(side, D)
    kv = call(slabs_body, [(slab, D)] * 4, 2 * slab * D * D * 4, 6 * MIB, n_in=5)(
        a.reshape(slab, D), b.reshape(slab, D), gain_s, spatial_key, spatial_value)
    middles, fars, partners = [], [], []
    for c in range(CHUNKS):
        (middle,) = call(
            functools.partial(window_body, c), [(part, D)], 10**9, 8 * MIB, n_in=14,
            scratch=[pltpu.VMEM((2 * PART * SIDE, D), BF), pltpu.VMEM((2 * PART * SIDE, D), BF), pltpu.VMEM((part, D), BF)],
        )(x, q, k, v, *kv, side_a, side_b, gain_s, spatial_key, spatial_value, spatial_output)
        middles.append(middle)
        fars.append(across(middle, 2))
        partners.append(across(middle, 1))
    big = jax.ShapeDtypeStruct((own, D), F32)
    rows = [pltpu.VMEM((own, D), BF)] * 4
    state = call(near_body, [(own, D), big, big, big], 4 * own * D * D * 5, 8 * MIB, n_in=2 * CHUNKS + 4, scratch=rows)(
        *middles, *partners, gain_t, temporal_query, temporal_key, temporal_value)
    keys, values = [], []
    for c in range(CHUNKS):
        forwarded = across(fars[c], 1)
        for value, label in ((fars[c], f"far{c}"), (forwarded, f"way{c}")):
            if label != f"way{CHUNKS - 1}":
                fk, fv = call(far_body, [(part, D)] * 2, 2 * part * D * D * 2, 3 * MIB, n_in=4)(
                    value, gain_t, temporal_key, temporal_value)
                keys.append(fk)
                values.append(fv)
    (refined,) = call(
        views_body, [(own, D)], 10**9, 8 * MIB, n_in=CHUNKS + 4 + 4 * CHUNKS - 2 + 5,
        scratch=[pltpu.VMEM((part, D), BF), pltpu.VMEM((part, D), BF), pltpu.VMEM((own, D), BF)],
    )(*middles, *state, *keys, *values, forwarded, gain_t, temporal_key, temporal_value, temporal_output)
    return refined.reshape(view_maps.shape)


def solution(mesh):
    return jax.shard_map(
        body,
        mesh=mesh,
        in_specs=(P("view", "row", "col", None), P(), P(), P(), P(), P(), P(), P(), P(), P(), P()),
        out_specs=P("view", "row", "col", None),
        check_vma=False,
    )
```

time: 51.2 us -> 50 us (0.977)
  waiting for transfers between devices: 11.6 us -> 7.21 us
  Pallas kernels: 11.7 us -> 14.5 us
    ppermute x7 -> x10, waiting for transfers between devices: 11.6 us -> 7.21 us  [the longest x4 6.42 us: swap(): return lax.ppermute(value, axis, pairs + [(j, i) for i, j in pairs])]
    pallas_call x6 -> x10, Pallas kernels: 11.7 us -> 14.5 us  [the longest x2 3.56 us: body(): call(functools.partial(window_body, c), [(part, D)], 10 ** 9, 8 * MIB, n_...]
    dynamic_slice x0 -> x1, local copies, waits for them, and re-layouts: none -> 1.21 us  [body(): b = swap(lax.dynamic_slice_in_dim(view_maps, odd, RADIUS, axis=1), 'row', 1)]
    slice x1 -> x0, local copies, waits for them, and re-layouts: 1.15 us -> none  [body(): down = lax.ppermute(view_maps[:, :RADIUS], 'row', backward)]
    unnamed x26 -> x24, local copies, waits for them, and re-layouts: 3.85 us -> 4.09 us
    ppermute x7 -> x10, starting transfers between devices: 22.3 us -> 22.3 us  [the longest x6 12.3 us: across(): return lax.ppermute(value, 'view', [(i, i ^ step) for i in range(4)])]
  transfers between devices with their start and end apart: 7 -> 10, of which waited for: 3 -> 3; matrix products, arithmetic and copies ran while one was open for 0% -> 0% of each run, Pallas kernels for 8% -> 18%
where the time goes in v2:
time: 50 us; the launch traced here: 49.6 us
  starting transfers between devices  22.3 us (45%)
  Pallas kernels  14.5 us (29%)
  waiting for transfers between devices  7.21 us (14%)
  local copies, waits for them, and re-layouts  5.32 us (11%)
    ppermute x6, starting transfers between devices, across(): return lax.ppermute(value, 'view', [(i, i ^ step) for i in range(4)])  12.3 us
    ppermute x4, starting transfers between devices, swap(): return lax.ppermute(value, axis, pairs + [(j, i) for i, j in pairs])  9.97 us
    ppermute x4, waiting for transfers between devices, swap(): return lax.ppermute(value, axis, pairs + [(j, i) for i, j in pairs])  6.42 us
    unnamed x24, local copies, waits for them, and re-layouts  4.09 us
    pallas_call x2, Pallas kernels, body(): call(functools.partial(window_body, c), [(part, D)], 10 ** 9, 8 * MIB, n_...  3.56 us
    pallas_call x1, Pallas kernels, body(): call(views_body, [(own, D)], 10 ** 9, 8 * MIB, n_in=CHUNKS + 4 + 4 * CHUN...  3.53 us
    pallas_call x1, Pallas kernels, body(): call(near_body, [(own, D), big, big, big], 4 * own * D * D * 5, 8 * MIB,...  3.14 us
    pallas_call x3, Pallas kernels, body(): call(far_body, [(part, D)] * 2, 2 * part * D * D * 2, 3 * MIB, n_in=4)  1.65 us
  transfers between devices with their start and end apart: 10, of which 3 were waited for; matrix products, arithmetic and copies ran while one was open for 0% of the time, Pallas kernels for 18%

profile of v2, /device:TPU:103, one launch (start us, length us, event | category | flops | bytes accessed | tf_op | source)
XLA Modules:
  0.0 49.6 jit_solution(9304524464565191942)
XLA Ops:
  0.0 0.0 copy-start.2
  0.0 0.0 copy-start.10
  0.0 0.0 copy-start.3
  0.0 1.2 %constant_dynamic-slice_fusion = (bf16[4,3,16,768]{3,2,1,0:T(8,128)(2,1)S(1)}, bf16[4,3,16,768]{3,2,1,0:T(8,128)(2,1)S(1)}) fusion(bf16[4,4,16,768]{3,2,1,0:T(8,128)(2,1)} %param.11, s32[]{:T(128)S(6)} %select_n.7, s32[]{:T(128)S(6)} %select_n.6), kind=kLoop, calls=%fused_computation | loop fusion | bytes 1179656 | tf_op jit(solution)/shard_map/dynamic_slice | solution.py:274
  1.2 0.1 collective-permute-start
  1.3 5.5 %collective-permute-start.1 = (bf16[4,3,16,768]{3,2,1,0:T(8,128)(2,1)S(1)}, bf16[4,3,16,768]{3,2,1,0:T(8,128)(2,1)S(1)}, u32[]{:S(2)}, u32[]{:S(2)}) collective-permute-start(bf16[4,3,16,768]{3,2,1,0:T(8,128)(2,1)S(1)} %get-tuple-element.43), channel_id=1, source_target_pairs={{8,16},{24,32},{40,48},{16,8},{32,24},{48,40},{9,17},{25,33},{41,4... | collective-permute-start | bytes 884744 | tf_op jit(solution)/shard_map/ppermute | solution.py:247
  6.8 2.4 %collective-permute-done = bf16[4,3,16,768]{3,2,1,0:T(8,128)(2,1)S(1)} collective-permute-done((bf16[4,3,16,768]{3,2,1,0:T(8,128)(2,1)S(1)}, bf16[4,3,16,768]{3,2,1,0:T(8,128)(2,1)S(1)}, u32[]{:S(2)}, u32[]{:S(2)}) %collective-permute-start) | collective-permute-done | bytes 294944 | tf_op jit(solution)/shard_map/ppermute | solution.py:247
  9.2 4.0 %collective-permute-done.1 = bf16[4,3,16,768]{3,2,1,0:T(8,128)(2,1)S(1)} collective-permute-done((bf16[4,3,16,768]{3,2,1,0:T(8,128)(2,1)S(1)}, bf16[4,3,16,768]{3,2,1,0:T(8,128)(2,1)S(1)}, u32[]{:S(2)}, u32[]{:S(2)}) %collective-permute-start.1) | collective-permute-done | bytes 294944 | tf_op jit(solution)/shard_map/ppermute | solution.py:247
  13.2 0.0 copy-done.2
  13.2 0.3 shard_map.111
  13.5 0.6 %collective-permute-start.2 = (bf16[4,32,768]{2,1,0:T(8,128)(2,1)S(1)}, bf16[4,32,768]{2,1,0:T(8,128)(2,1)S(1)}, u32[]{:S(2)}, u32[]{:S(2)}) collective-permute-start(bf16[4,32,768]{2,1,0:T(8,128)(2,1)S(1)} %get-tuple-element.31), channel_id=1, source_target_pairs={{0,1},{2,3},{4,5},{6,7},{1,0},{3,2},{5,4},{7,6},{8,9},{10,11},{12,... | collective-permute-start | bytes 589832 | tf_op jit(solution)/shard_map/ppermute | solution.py:247
  14.2 3.8 %collective-permute-start.3 = (bf16[4,32,768]{2,1,0:T(8,128)(2,1)S(1)}, bf16[4,32,768]{2,1,0:T(8,128)(2,1)S(1)}, u32[]{:S(2)}, u32[]{:S(2)}) collective-permute-start(bf16[4,32,768]{2,1,0:T(8,128)(2,1)S(1)} %get-tuple-element.32), channel_id=1, source_target_pairs={{1,2},{3,4},{5,6},{2,1},{4,3},{6,5},{9,10},{11,12},{13,14},{10,9},... | collective-permute-start | bytes 589832 | tf_op jit(solution)/shard_map/ppermute | solution.py:247
  17.9 0.0 copy-done.10
  18.0 0.0 copy-done.3
  18.0 0.0 copy-start.4
  18.0 1.3 %copy-done.4 = bf16[768,768]{1,0:T(8,128)(2,1)S(1)} copy-done((bf16[768,768]{1,0:T(8,128)(2,1)S(1)}, bf16[768,768]{1,0:T(8,128)(2,1)}, u32[]{:S(2)}) %copy-start.4) | copy-done | bytes 1179672
  19.2 0.0 copy-start.8
  19.2 1.3 %copy-done.8 = bf16[768,768]{1,0:T(8,128)(2,1)S(1)} copy-done((bf16[768,768]{1,0:T(8,128)(2,1)S(1)}, bf16[768,768]{1,0:T(8,128)(2,1)}, u32[]{:S(2)}) %copy-start.8) | copy-done | bytes 1179672
  20.5 0.0 copy-start.5
  20.5 1.2 %shard_map.109 = (bf16[256,768]{1,0:T(8,128)(2,1)S(1)}, bf16[256,768]{1,0:T(8,128)(2,1)S(1)}, bf16[256,768]{1,0:T(8,128)(2,1)S(1)}) custom-call(bf16[256,768]{1,0:T(8,128)(2,1)S(1)} %bitcast.9, f32[1,768]{1,0:T(1,128)S(1)} %reshape.31.gain, bf16[768,768]{1,0:T(8,128)(2,1)S(1)} %copy-done.8, bf16[768,768]{1,0:T(8,128)(2,1)S(1)} %copy-done.3, ...), custom_call_target="tpu_custom_call" | custom-call | flops 905969664 | bytes 6291456 | tf_op jit(solution)/shard_map/pallas_call | solution.py:275
  21.7 0.1 copy-done.5
  21.8 0.0 copy-start.6
  21.8 1.2 %shard_map.110 = (bf16[192,768]{1,0:T(8,128)(2,1)S(1)}, bf16[192,768]{1,0:T(8,128)(2,1)S(1)}, bf16[192,768]{1,0:T(8,128)(2,1)S(1)}, bf16[192,768]{1,0:T(8,128)(2,1)S(1)}) custom-call(bf16[192,768]{1,0:T(8,128)(2,1)S(1)} %bitcast.17, bf16[192,768]{1,0:T(8,128)(2,1)S(1)} %bitcast.19, f32[1,768]{1,0:T(1,128)S(1)} %reshape.31.gain, ...), custom_call_target="tpu_custom_call" | custom-call | flops 905969664 | bytes 6291456 | tf_op jit(solution)/shard_map/pallas_call | solution.py:282
  23.0 0.0 collective-permute-done.2
  23.0 0.0 collective-permute-done.3
  23.0 0.1 copy-done.6
  23.1 1.8 %shard_map.112.refs_0_ = bf16[128,768]{1,0:T(8,128)(2,1)S(1)} custom-call(bf16[256,768]{1,0:T(8,128)(2,1)S(1)} %bitcast.10, bf16[256,768]{1,0:T(8,128)(2,1)S(1)} %get-tuple-element.24.q, bf16[256,768]{1,0:T(8,128)(2,1)S(1)} %get-tuple-element.25.k, bf16[256,768]{1,0:T(8,128)(2,1)S(1)} %get-tuple-element.26.v, bf16[192,768]{1,0:T(8,128)(2,1)S(1)} %get-tuple-element.27.ka, ...), custom_call_target="tpu_custom_call" | custom-call | flops 1000000000 | bytes 8388608 | tf_op jit(solution)/shard_map/pallas_call | solution.py:286
  24.8 0.0 copy-start.11
  24.9 0.0 copy-start
  24.9 0.0 copy-start.1
  24.9 2.7 %collective-permute-start.6 = (bf16[128,768]{1,0:T(8,128)(2,1)S(1)}, bf16[128,768]{1,0:T(8,128)(2,1)S(1)}, u32[]{:S(2)}, u32[]{:S(2)}) collective-permute-start(bf16[128,768]{1,0:T(8,128)(2,1)S(1)} %shard_map.112.refs_0_), channel_id=1, source_target_pairs={{0,128},{64,192},{128,0},{192,64},{1,129},{65,193},{129,1},{193,65... | collective-permute-start | bytes 589832 | tf_op jit(solution)/shard_map/ppermute | solution.py:251
  27.6 1.8 %shard_map.113.refs_1_ = bf16[128,768]{1,0:T(8,128)(2,1)S(1)} custom-call(bf16[256,768]{1,0:T(8,128)(2,1)S(1)} %bitcast.11, bf16[256,768]{1,0:T(8,128)(2,1)S(1)} %get-tuple-element.24.q, bf16[256,768]{1,0:T(8,128)(2,1)S(1)} %get-tuple-element.25.k, bf16[256,768]{1,0:T(8,128)(2,1)S(1)} %get-tuple-element.26.v, bf16[192,768]{1,0:T(8,128)(2,1)S(1)} %get-tuple-element.27.ka, ...), custom_call_target="tpu_custom_call" | custom-call | flops 1000000000 | bytes 8388608 | tf_op jit(solution)/shard_map/pallas_call | solution.py:286
  29.4 0.4 collective-permute-start.8
  29.8 3.1 %collective-permute-start.5 = (bf16[128,768]{1,0:T(8,128)(2,1)S(1)}, bf16[128,768]{1,0:T(8,128)(2,1)S(1)}, u32[]{:S(2)}, u32[]{:S(2)}) collective-permute-start(bf16[128,768]{1,0:T(8,128)(2,1)S(1)} %shard_map.113.refs_1_), channel_id=1, source_target_pairs={{0,64},{64,0},{128,192},{192,128},{1,65},{65,1},{129,193},{193,129... | collective-permute-start | bytes 589832 | tf_op jit(solution)/shard_map/ppermute | solution.py:251
  32.9 0.0 collective-permute-start.4
  33.0 0.0 copy-done.11
  33.0 0.0 collective-permute-done.6.far
  33.0 2.4 %collective-permute-start.7 = (bf16[128,768]{1,0:T(8,128)(2,1)S(1)}, bf16[128,768]{1,0:T(8,128)(2,1)S(1)}, u32[]{:S(2)}, u32[]{:S(2)}) collective-permute-start(bf16[128,768]{1,0:T(8,128)(2,1)S(1)} %collective-permute-done.6.far), channel_id=1, source_target_pairs={{0,64},{64,0},{128,192},{192,128},{1,65},{65,1},{129,193},{193,129... | collective-permute-start | bytes 589832 | tf_op jit(solution)/shard_map/ppermute | solution.py:251
  35.4 0.8 %collective-permute-done.8.far = bf16[128,768]{1,0:T(8,128)(2,1)S(1)} collective-permute-done((bf16[128,768]{1,0:T(8,128)(2,1)S(1)}, bf16[128,768]{1,0:T(8,128)(2,1)S(1)}, u32[]{:S(2)}, u32[]{:S(2)}) %collective-permute-start.8) | collective-permute-done | bytes 196640 | tf_op jit(solution)/shard_map/ppermute | solution.py:251
  36.1 3.7 %collective-permute-start.9 = (bf16[128,768]{1,0:T(8,128)(2,1)S(1)}, bf16[128,768]{1,0:T(8,128)(2,1)S(1)}, u32[]{:S(2)}, u32[]{:S(2)}) collective-permute-start(bf16[128,768]{1,0:T(8,128)(2,1)S(1)} %collective-permute-done.8.far), channel_id=1, source_target_pairs={{0,64},{64,0},{128,192},{192,128},{1,65},{65,1},{129,193},{193,129... | collective-permute-start | bytes 589832 | tf_op jit(solution)/shard_map/ppermute | solution.py:251
  39.8 0.0 copy-done
  39.8 0.0 copy-done.1
  39.8 0.5 %shard_map.117 = (bf16[128,768]{1,0:T(8,128)(2,1)S(1)}, bf16[128,768]{1,0:T(8,128)(2,1)S(1)}) custom-call(bf16[128,768]{1,0:T(8,128)(2,1)S(1)} %collective-permute-done.8.far, f32[1,768]{1,0:T(1,128)S(1)} %reshape.38.refs_4_.gain.refs_13_, bf16[768,768]{1,0:T(8,128)(2,1)S(1)} %copy-done, bf16[768,768]{1,0:T(8,128)(2,1)S(1)} %copy-done.1), custom_call_target="tpu_custom_call" | custom-call | flops 301989888 | bytes 3145728 | tf_op jit(solution)/shard_map/pallas_call | solution.py:302
  40.4 0.0 copy-start.9
  40.4 0.6 %shard_map.115 = (bf16[128,768]{1,0:T(8,128)(2,1)S(1)}, bf16[128,768]{1,0:T(8,128)(2,1)S(1)}) custom-call(bf16[128,768]{1,0:T(8,128)(2,1)S(1)} %collective-permute-done.6.far, f32[1,768]{1,0:T(1,128)S(1)} %reshape.38.refs_4_.gain.refs_13_, bf16[768,768]{1,0:T(8,128)(2,1)S(1)} %copy-done, bf16[768,768]{1,0:T(8,128)(2,1)S(1)} %copy-done.1), custom_call_target="tpu_custom_call" | custom-call | flops 301989888 | bytes 3145728 | tf_op jit(solution)/shard_map/pallas_call | solution.py:302
  40.9 0.0 collective-permute-done.5.refs_3_
  41.0 0.0 collective-permute-done.4.refs_2_
  41.0 0.7 %copy-done.9 = bf16[768,768]{1,0:T(8,128)(2,1)S(1)} copy-done((bf16[768,768]{1,0:T(8,128)(2,1)S(1)}, bf16[768,768]{1,0:T(8,128)(2,1)}, u32[]{:S(2)}) %copy-start.9) | copy-done | bytes 1179672
  41.6 3.1 %shard_map.114 = (bf16[256,768]{1,0:T(8,128)(2,1)S(1)}, f32[256,768]{1,0:T(8,128)S(1)}, f32[256,768]{1,0:T(8,128)S(1)}, f32[256,768]{1,0:T(8,128)S(1)}) custom-call(bf16[128,768]{1,0:T(8,128)(2,1)S(1)} %shard_map.112.refs_0_, bf16[128,768]{1,0:T(8,128)(2,1)S(1)} %shard_map.113.refs_1_, bf16[128,768]{1,0:T(8,128)(2,1)S(1)} %collective-permute-done.4.refs_2_, ...), custom_call_target="tpu_custom_call" | custom-call | flops 3019898880 | bytes 8388608 | tf_op jit(solution)/shard_map/pallas_call | solution.py:295
  44.8 0.0 copy-start.7
  44.8 0.0 collective-permute-done.7.far
  44.8 0.6 %shard_map.116 = (bf16[128,768]{1,0:T(8,128)(2,1)S(1)}, bf16[128,768]{1,0:T(8,128)(2,1)S(1)}) custom-call(bf16[128,768]{1,0:T(8,128)(2,1)S(1)} %collective-permute-done.7.far, f32[1,768]{1,0:T(1,128)S(1)} %reshape.38.refs_4_.gain.refs_13_, bf16[768,768]{1,0:T(8,128)(2,1)S(1)} %copy-done, bf16[768,768]{1,0:T(8,128)(2,1)S(1)} %copy-done.1), custom_call_target="tpu_custom_call" | custom-call | flops 301989888 | bytes 3145728 | tf_op jit(solution)/shard_map/pallas_call | solution.py:302
  45.4 0.0 collective-permute-done.9.refs_12_
  45.4 0.7 %copy-done.7 = bf16[768,768]{1,0:T(8,128)(2,1)S(1)} copy-done((bf16[768,768]{1,0:T(8,128)(2,1)S(1)}, bf16[768,768]{1,0:T(8,128)(2,1)}, u32[]{:S(2)}) %copy-start.7) | copy-done | bytes 1179672
  46.1 3.5 %shard_map.118 = bf16[256,768]{1,0:T(8,128)(2,1)} custom-call(bf16[128,768]{1,0:T(8,128)(2,1)S(1)} %shard_map.112.refs_0_, bf16[128,768]{1,0:T(8,128)(2,1)S(1)} %shard_map.113.refs_1_, bf16[256,768]{1,0:T(8,128)(2,1)S(1)} %get-tuple-element.33.refs_2_, f32[256,768]{1,0:T(8,128)S(1)} %get-tuple-element.34.refs_3_, f32[256,768]{1,0:T(8,128)S(1)} %get-tuple-element.35.refs_4_, ...), custom_call_target="tpu_custom_call" | custom-call | flops 1000000000 | bytes 8388608 | tf_op jit(solution)/shard_map/pallas_call | solution.py:306
  (2 shorter events, 0.0 us)
Async XLA Ops:
  0.0 13.2 %copy-start.2 = (bf16[4,4,16,768]{3,2,1,0:T(8,128)(2,1)S(1)}, bf16[4,4,16,768]{3,2,1,0:T(8,128)(2,1)}, u32[]{:S(2)}) copy-start(bf16[4,4,16,768]{3,2,1,0:T(8,128)(2,1)} %param.11) | copy-start | bytes 1179652
  0.0 17.9 %copy-start.10 = (f32[768]{0:T(1024)S(1)}, f32[768]{0:T(1024)}, u32[]{:S(2)}) copy-start(f32[768]{0:T(1024)} %param.12) | copy-start | bytes 9220
  0.0 18.0 %copy-start.3 = (bf16[768,768]{1,0:T(8,128)(2,1)S(1)}, bf16[768,768]{1,0:T(8,128)(2,1)}, u32[]{:S(2)}) copy-start(bf16[768,768]{1,0:T(8,128)(2,1)} %wk.10) | copy-start | bytes 3538948
  1.2 8.0 %collective-permute-start = (bf16[4,3,16,768]{3,2,1,0:T(8,128)(2,1)S(1)}, bf16[4,3,16,768]{3,2,1,0:T(8,128)(2,1)S(1)}, u32[]{:S(2)}, u32[]{:S(2)}) collective-permute-start(bf16[4,3,16,768]{3,2,1,0:T(8,128)(2,1)S(1)} %get-tuple-element.44), channel_id=1, source_target_pairs={{0,8},{16,24},{32,40},{48,56},{8,0},{24,16},{40,32},{56,48},{1,9},... | collective-permute-start | bytes 884744 | tf_op jit(solution)/shard_map/ppermute | solution.py:247
  1.3 11.9 %collective-permute-start.1 = (bf16[4,3,16,768]{3,2,1,0:T(8,128)(2,1)S(1)}, bf16[4,3,16,768]{3,2,1,0:T(8,128)(2,1)S(1)}, u32[]{:S(2)}, u32[]{:S(2)}) collective-permute-start(bf16[4,3,16,768]{3,2,1,0:T(8,128)(2,1)S(1)} %get-tuple-element.43), channel_id=1, source_target_pairs={{8,16},{24,32},{40,48},{16,8},{32,24},{48,40},{9,17},{25,33},{41,4... | collective-permute-start | bytes 884744 | tf_op jit(solution)/shard_map/ppermute | solution.py:247
  13.5 9.4 %collective-permute-start.2 = (bf16[4,32,768]{2,1,0:T(8,128)(2,1)S(1)}, bf16[4,32,768]{2,1,0:T(8,128)(2,1)S(1)}, u32[]{:S(2)}, u32[]{:S(2)}) collective-permute-start(bf16[4,32,768]{2,1,0:T(8,128)(2,1)S(1)} %get-tuple-element.31), channel_id=1, source_target_pairs={{0,1},{2,3},{4,5},{6,7},{1,0},{3,2},{5,4},{7,6},{8,9},{10,11},{12,... | collective-permute-start | bytes 589832 | tf_op jit(solution)/shard_map/ppermute | solution.py:247
  14.2 8.8 %collective-permute-start.3 = (bf16[4,32,768]{2,1,0:T(8,128)(2,1)S(1)}, bf16[4,32,768]{2,1,0:T(8,128)(2,1)S(1)}, u32[]{:S(2)}, u32[]{:S(2)}) collective-permute-start(bf16[4,32,768]{2,1,0:T(8,128)(2,1)S(1)} %get-tuple-element.32), channel_id=1, source_target_pairs={{1,2},{3,4},{5,6},{2,1},{4,3},{6,5},{9,10},{11,12},{13,14},{10,9},... | collective-permute-start | bytes 589832 | tf_op jit(solution)/shard_map/ppermute | solution.py:247
  18.0 1.3 %copy-start.4 = (bf16[768,768]{1,0:T(8,128)(2,1)S(1)}, bf16[768,768]{1,0:T(8,128)(2,1)}, u32[]{:S(2)}) copy-start(bf16[768,768]{1,0:T(8,128)(2,1)} %wv.10) | copy-start | bytes 3538948
  19.2 1.3 %copy-start.8 = (bf16[768,768]{1,0:T(8,128)(2,1)S(1)}, bf16[768,768]{1,0:T(8,128)(2,1)}, u32[]{:S(2)}) copy-start(bf16[768,768]{1,0:T(8,128)(2,1)} %wq.1) | copy-start | bytes 3538948
  20.5 1.3 %copy-start.5 = (bf16[768,768]{1,0:T(8,128)(2,1)S(1)}, bf16[768,768]{1,0:T(8,128)(2,1)}, u32[]{:S(2)}) copy-start(bf16[768,768]{1,0:T(8,128)(2,1)} %wv.10) | copy-start | bytes 3538948
  21.8 1.3 %copy-start.6 = (bf16[768,768]{1,0:T(8,128)(2,1)S(1)}, bf16[768,768]{1,0:T(8,128)(2,1)}, u32[]{:S(2)}) copy-start(bf16[768,768]{1,0:T(8,128)(2,1)} %wo.3) | copy-start | bytes 3538948
  24.8 8.1 %copy-start.11 = (f32[768]{0:T(1024)S(1)}, f32[768]{0:T(1024)}, u32[]{:S(2)}) copy-start(f32[768]{0:T(1024)} %param.17) | copy-start | bytes 9220
  24.9 14.9 %copy-start = (bf16[768,768]{1,0:T(8,128)(2,1)S(1)}, bf16[768,768]{1,0:T(8,128)(2,1)}, u32[]{:S(2)}) copy-start(bf16[768,768]{1,0:T(8,128)(2,1)} %refs_14_.1) | copy-start | bytes 3538948
  24.9 14.9 %copy-start.1 = (bf16[768,768]{1,0:T(8,128)(2,1)S(1)}, bf16[768,768]{1,0:T(8,128)(2,1)}, u32[]{:S(2)}) copy-start(bf16[768,768]{1,0:T(8,128)(2,1)} %refs_15_.1) | copy-start | bytes 3538948
  24.9 8.1 %collective-permute-start.6 = (bf16[128,768]{1,0:T(8,128)(2,1)S(1)}, bf16[128,768]{1,0:T(8,128)(2,1)S(1)}, u32[]{:S(2)}, u32[]{:S(2)}) collective-permute-start(bf16[128,768]{1,0:T(8,128)(2,1)S(1)} %shard_map.112.refs_0_), channel_id=1, source_target_pairs={{0,128},{64,192},{128,0},{192,64},{1,129},{65,193},{129,1},{193,65... | collective-permute-start | bytes 589832 | tf_op jit(solution)/shard_map/ppermute | solution.py:251
  29.4 6.8 %collective-permute-start.8 = (bf16[128,768]{1,0:T(8,128)(2,1)S(1)}, bf16[128,768]{1,0:T(8,128)(2,1)S(1)}, u32[]{:S(2)}, u32[]{:S(2)}) collective-permute-start(bf16[128,768]{1,0:T(8,128)(2,1)S(1)} %shard_map.113.refs_1_), channel_id=1, source_target_pairs={{0,128},{64,192},{128,0},{192,64},{1,129},{65,193},{129,1},{193,65... | collective-permute-start | bytes 589832 | tf_op jit(solution)/shard_map/ppermute | solution.py:251
  29.8 11.1 %collective-permute-start.5 = (bf16[128,768]{1,0:T(8,128)(2,1)S(1)}, bf16[128,768]{1,0:T(8,128)(2,1)S(1)}, u32[]{:S(2)}, u32[]{:S(2)}) collective-permute-start(bf16[128,768]{1,0:T(8,128)(2,1)S(1)} %shard_map.113.refs_1_), channel_id=1, source_target_pairs={{0,64},{64,0},{128,192},{192,128},{1,65},{65,1},{129,193},{193,129... | collective-permute-start | bytes 589832 | tf_op jit(solution)/shard_map/ppermute | solution.py:251
  32.9 8.0 %collective-permute-start.4 = (bf16[128,768]{1,0:T(8,128)(2,1)S(1)}, bf16[128,768]{1,0:T(8,128)(2,1)S(1)}, u32[]{:S(2)}, u32[]{:S(2)}) collective-permute-start(bf16[128,768]{1,0:T(8,128)(2,1)S(1)} %shard_map.112.refs_0_), channel_id=1, source_target_pairs={{0,64},{64,0},{128,192},{192,128},{1,65},{65,1},{129,193},{193,129... | collective-permute-start | bytes 589832 | tf_op jit(solution)/shard_map/ppermute | solution.py:251
  33.0 11.8 %collective-permute-start.7 = (bf16[128,768]{1,0:T(8,128)(2,1)S(1)}, bf16[128,768]{1,0:T(8,128)(2,1)S(1)}, u32[]{:S(2)}, u32[]{:S(2)}) collective-permute-start(bf16[128,768]{1,0:T(8,128)(2,1)S(1)} %collective-permute-done.6.far), channel_id=1, source_target_pairs={{0,64},{64,0},{128,192},{192,128},{1,65},{65,1},{129,193},{193,129... | collective-permute-start | bytes 589832 | tf_op jit(solution)/shard_map/ppermute | solution.py:251
  36.1 9.2 %collective-permute-start.9 = (bf16[128,768]{1,0:T(8,128)(2,1)S(1)}, bf16[128,768]{1,0:T(8,128)(2,1)S(1)}, u32[]{:S(2)}, u32[]{:S(2)}) collective-permute-start(bf16[128,768]{1,0:T(8,128)(2,1)S(1)} %collective-permute-done.8.far), channel_id=1, source_target_pairs={{0,64},{64,0},{128,192},{192,128},{1,65},{65,1},{129,193},{193,129... | collective-permute-start | bytes 589832 | tf_op jit(solution)/shard_map/ppermute | solution.py:251
  40.4 1.3 %copy-start.9 = (bf16[768,768]{1,0:T(8,128)(2,1)S(1)}, bf16[768,768]{1,0:T(8,128)(2,1)}, u32[]{:S(2)}) copy-start(bf16[768,768]{1,0:T(8,128)(2,1)} %refs_5_.1) | copy-start | bytes 3538948
  44.8 1.3 %copy-start.7 = (bf16[768,768]{1,0:T(8,128)(2,1)S(1)}, bf16[768,768]{1,0:T(8,128)(2,1)}, u32[]{:S(2)}) copy-start(bf16[768,768]{1,0:T(8,128)(2,1)} %refs_16_.1) | copy-start | bytes 3538948

commit v3 on v2

v3 whole, which is shorter than its diff:
```python
import functools

import jax
import jax.numpy as jnp
from jax import lax
from jax.experimental import pallas as pl
from jax.experimental.pallas import tpu as pltpu
from jax.sharding import PartitionSpec as P


HEADS = 12
HEAD_DIM = 64
RADIUS = 3
CHUNKS = 2
D = 768
GROUP = 4
LANES = GROUP * HEAD_DIM
GROUPS = HEADS // GROUP
ROWS = 4
COLS = 16
TOKENS = ROWS * COLS
SLAB = RADIUS * COLS
SIDE = 32
EDGE = ROWS * RADIUS
CORNER = 2 * RADIUS * RADIUS
KEYS = TOKENS + 2 * SLAB + 2 * SIDE
VIEWS = 4
PART = VIEWS // CHUNKS
ALL_VIEWS = 16
MAP_H = 32
MAP_W = 128

epsilon = 1e-06
very_negative = -1e30
BF = jnp.bfloat16
F32 = jnp.float32
MIB = 1 << 20


def call(body, outs, flops, nbytes, scratch=(), n_in=0, limit=20):
    vmem = pl.BlockSpec(memory_space=pltpu.VMEM)
    return pl.pallas_call(
        body,
        out_shape=tuple(jax.ShapeDtypeStruct(s, BF) if isinstance(s, tuple) else s for s in outs),
        in_specs=[vmem] * n_in,
        out_specs=tuple(vmem for _ in outs),
        scratch_shapes=list(scratch),
        compiler_params=pltpu.CompilerParams(vmem_limit_bytes=limit * MIB),
        cost_estimate=pl.CostEstimate(flops=flops, bytes_accessed=nbytes, transcendentals=0),
    )


def rows_body(maps, a, b, sems):
    odd = lax.axis_index("row") & 1
    copies = [
        pltpu.make_async_copy(maps.at[:, pl.ds(1 - odd, RADIUS)], a, sems.at[0]),
        pltpu.make_async_copy(maps.at[:, pl.ds(odd, RADIUS)], b, sems.at[1]),
    ]
    for copy in copies:
        copy.start()
    for copy in copies:
        copy.wait()


def normed(tokens, gain):
    values = tokens.astype(F32)
    mean = jnp.mean(values * values, axis=-1, keepdims=True)
    return (values * lax.rsqrt(mean + epsilon) * gain[None, :]).astype(BF)


def dot(a, b):
    return jnp.dot(a, b, preferred_element_type=F32)


def own_body(x, gain, wq, q):
    q[...] = (dot(normed(x[...], gain[...]), wq[...]).astype(BF) * 0.125).astype(BF)


def side_base(second):
    odd = lax.axis_index("col") & 1
    return jnp.where(second == (odd == 1), COLS - RADIUS, 0)


def edges_body(x, to_a, to_b):
    shape = (2 * VIEWS * EDGE, VIEWS * TOKENS)
    i = lax.broadcasted_iota(jnp.int32, shape, 0)
    j = lax.broadcasted_iota(jnp.int32, shape, 1)
    second = i >= VIEWS * EDGE
    col = (j & 15) - side_base(second)
    place = EDGE * (j >> 6) + RADIUS * ((j >> 4) & 3) + col + jnp.where(second, VIEWS * EDGE, 0)
    pick = jnp.where((col >= 0) & (col < RADIUS) & (i == place), 1.0, 0.0).astype(BF)
    taken = dot(pick, x[...]).astype(BF)
    to_a[...] = taken[:VIEWS * EDGE]
    to_b[...] = taken[VIEWS * EDGE:]


def corners_body(a, b, to_a, to_b):
    shape = (2 * VIEWS * CORNER, VIEWS * SLAB)
    i = lax.broadcasted_iota(jnp.int32, shape, 0)
    j = lax.broadcasted_iota(jnp.int32, shape, 1)
    second = i >= VIEWS * CORNER
    col = (j & 15) - side_base(second)
    line = j >> 4
    view = (line * 43) >> 7
    place = CORNER * view + RADIUS * (line - RADIUS * view) + col + jnp.where(second, VIEWS * CORNER, 0)
    good = (col >= 0) & (col < RADIUS)
    half = CORNER // 2
    pick_a = jnp.where(good & (i == place), 1.0, 0.0).astype(BF)
    pick_b = jnp.where(good & (i == place + half), 1.0, 0.0).astype(BF)
    taken = (dot(pick_a, a[...]) + dot(pick_b, b[...])).astype(BF)
    to_a[...] = taken[:VIEWS * CORNER]
    to_b[...] = taken[VIEWS * CORNER:]


def slabs_body(x, a, b, gain, wk, wv, k, v, ka, va, kb, vb):
    for source, key, value in ((x, k, v), (a, ka, va), (b, kb, vb)):
        n = normed(source[...], gain[...])
        key[...] = dot(n, wk[...]).astype(BF)
        value[...] = dot(n, wv[...]).astype(BF)


def compact(full, spread):
    full = jnp.where(spread, full, 0.0)
    count = full.shape[0] // GROUP
    result = full[:count]
    for head in range(1, GROUP):
        result = result + full[head * count:(head + 1) * count]
    return result


def attend(q, keys, values, allowed, spread):
    stacked = jnp.concatenate([q] * GROUP, axis=0)
    stacked = jnp.where(spread, stacked, jnp.zeros_like(stacked))
    scores = lax.dot_general(stacked, keys, (((1,), (1,)), ((), ())), preferred_element_type=F32)
    scores = jnp.where(allowed, scores, very_negative)
    highest = jnp.max(scores, axis=-1, keepdims=True)
    weights = jnp.exp(scores - highest)
    share = 1.0 / jnp.sum(weights, axis=-1, keepdims=True)
    return compact(dot(weights.astype(BF), values) * share, spread).astype(BF)


def spread_mask(count):
    shape = (GROUP * count, LANES)
    row = lax.broadcasted_iota(jnp.int32, shape, 0)
    lane = lax.broadcasted_iota(jnp.int32, shape, 1)
    return (row // count) == (lane // HEAD_DIM)


def window_mask(first_row, first_col):
    flat = (1, KEYS)
    j = lax.broadcasted_iota(jnp.int32, flat, 1)
    odd_row = ((first_row >> 2) & 1) == 1
    odd_col = ((first_col >> 4) & 1) == 1
    base_a = jnp.where(odd_row, -RADIUS, ROWS)
    base_b = jnp.where(odd_row, ROWS, -RADIUS)
    slab_a, slab_b, side_a, side_b = TOKENS, TOKENS + SLAB, TOKENS + 2 * SLAB, TOKENS + 2 * SLAB + SIDE
    row = jnp.where(j < slab_a, j >> 4, jnp.where(j < slab_b, ((j - slab_a) >> 4) + base_a, ((j - slab_b) >> 4) + base_b))
    t = (j - side_a) & (SIDE - 1)
    t_row = (t * 43) >> 7
    t_col = t - RADIUS * t_row
    wide_row = jnp.where(t_row < RADIUS, t_row + base_a, jnp.where(t_row < RADIUS + ROWS, t_row - RADIUS, t_row - RADIUS - ROWS + base_b))
    side = j >= side_a
    row = jnp.where(side, wide_row, row)
    at_right = (j >= side_b) == odd_col
    col = jnp.where(side, jnp.where(at_right, t_col + COLS, t_col - RADIUS), j & 15)
    real = jnp.logical_not(side) | (t < RADIUS * (ROWS + 2 * RADIUS))
    there_row, there_col = first_row + row, first_col + col
    inside = (there_row >= 0) & (there_row < MAP_H) & (there_col >= 0) & (there_col < MAP_W)
    row = jnp.where(real & inside, row, 1000)
    shape = (TOKENS, KEYS)
    i = lax.broadcasted_iota(jnp.int32, shape, 0)
    near = (jnp.abs(row - (i >> 4)) <= RADIUS) & (jnp.abs(col - (i & 15)) <= RADIUS)
    tall = jnp.concatenate([near.astype(jnp.int32)] * GROUP, axis=0)
    return tall > 0


def side_tokens(first, edge_a, edge_b, corner_a, corner_b):
    stacked = jnp.concatenate([edge_a[...], edge_b[...], corner_a[...], corner_b[...]], axis=0)
    shape = (PART * 2 * SIDE, 2 * VIEWS * (EDGE + CORNER))
    i = lax.broadcasted_iota(jnp.int32, shape, 0)
    j = lax.broadcasted_iota(jnp.int32, shape, 1)
    view, part, t = (i >> 6) + first, (i >> 5) & 1, i & (SIDE - 1)
    upper, lower = t < RADIUS * RADIUS, t >= RADIUS * (RADIUS + ROWS)
    corner = 2 * VIEWS * EDGE + part * VIEWS * CORNER + view * CORNER + t
    edge = part * VIEWS * EDGE + view * EDGE + t - RADIUS * RADIUS
    source = jnp.where(upper, corner, jnp.where(lower, corner - EDGE, edge))
    pick = jnp.where((j == source) & (t < RADIUS * (ROWS + 2 * RADIUS)), 1.0, 0.0).astype(BF)
    return dot(pick, stacked).astype(BF)


def window_body(chunk, x, q, k, v, ka, va, kb, vb, edge_a, edge_b, corner_a, corner_b, gain, wk, wv, wo, middle, side_k, side_v, out):
    first = chunk * PART
    sides = normed(side_tokens(first, edge_a, edge_b, corner_a, corner_b), gain[...])
    side_k[...] = dot(sides, wk[...]).astype(BF)
    side_v[...] = dot(sides, wv[...]).astype(BF)
    allowed = window_mask(lax.axis_index("row") * ROWS, lax.axis_index("col") * COLS)
    spread = spread_mask(TOKENS)
    for view in range(PART):
        o = slice(view * TOKENS, (view + 1) * TOKENS)
        t = slice((first + view) * TOKENS, (first + view + 1) * TOKENS)
        s = slice((first + view) * SLAB, (first + view + 1) * SLAB)
        e = slice(view * 2 * SIDE, (view + 1) * 2 * SIDE)
        for group in range(GROUPS):
            f = slice(group * LANES, (group + 1) * LANES)
            keys = jnp.concatenate([k[t, f], ka[s, f], kb[s, f], side_k[e, f]], axis=0)
            values = jnp.concatenate([v[t, f], va[s, f], vb[s, f], side_v[e, f]], axis=0)
            out[o, f] = attend(q[t, f], keys, values, allowed, spread)
    middle[...] = (x[first * TOKENS:(first + PART) * TOKENS].astype(F32) + dot(out[...], wo[...])).astype(BF)


def same_place(count):
    shape = (GROUP * TOKENS, count)
    i = lax.broadcasted_iota(jnp.int32, shape, 0)
    j = lax.broadcasted_iota(jnp.int32, shape, 1)
    return (i & 15) == (j & 15)


def row_of(refs, row, f):
    return jnp.concatenate(
        [ref[w * TOKENS + row * COLS:w * TOKENS + (row + 1) * COLS, f] for ref in refs for w in range(ref.shape[0] // TOKENS)],
        axis=0,
    )


def near_body(*refs):
    middles = refs[:CHUNKS]
    gain, wq, wk, wv, q, k, v = refs[CHUNKS:]
    n = normed(jnp.concatenate([r[...] for r in middles], axis=0), gain[...])
    q[...] = (dot(n, wq[...]).astype(BF) * 0.125).astype(BF)
    k[...] = dot(n, wk[...]).astype(BF)
    v[...] = dot(n, wv[...]).astype(BF)


def pair_body(*refs):
    partners = refs[:CHUNKS]
    gain, wk, wv, kp, vp = refs[CHUNKS:]
    n = normed(jnp.concatenate([r[...] for r in partners], axis=0), gain[...])
    kp[...] = dot(n, wk[...]).astype(BF)
    vp[...] = dot(n, wv[...]).astype(BF)


def far_body(far, gain, wk, wv, k, v):
    n = normed(far[...], gain[...])
    k[...] = dot(n, wk[...]).astype(BF)
    v[...] = dot(n, wv[...]).astype(BF)


def views_body(*refs):
    middles, q = refs[:CHUNKS], refs[CHUNKS]
    refs = refs[CHUNKS + 1:]
    count = 2 * CHUNKS + 1
    keys, values = list(refs[:count]), list(refs[count:2 * count])
    last, gain, wk, wv, wo, refined, kl, vl, out = refs[2 * count:]
    far_body(last, gain, wk, wv, kl, vl)
    keys.append(kl)
    values.append(vl)
    spread = spread_mask(TOKENS)
    allowed = same_place(ALL_VIEWS * COLS)
    for row in range(ROWS):
        for group in range(GROUPS):
            f = slice(group * LANES, (group + 1) * LANES)
            full = attend(row_of([q], row, f), row_of(keys, row, f), row_of(values, row, f), allowed, spread)
            for w in range(VIEWS):
                out[w * TOKENS + row * COLS:w * TOKENS + (row + 1) * COLS, f] = full[w * COLS:(w + 1) * COLS]
    middle = jnp.concatenate([r[...] for r in middles], axis=0)
    refined[...] = (middle.astype(F32) + dot(out[...], wo[...])).astype(BF)


def swap(value, axis, first):
    count = lax.axis_size(axis)
    pairs = [(i, i + 1) for i in range(first, count - 1, 2)]
    return lax.ppermute(value, axis, pairs + [(j, i) for i, j in pairs])


def across(value, step):
    return lax.ppermute(value, "view", [(i, i ^ step) for i in range(4)])


def body(
    view_maps,
    gain_spatial,
    spatial_query,
    spatial_key,
    spatial_value,
    spatial_output,
    gain_temporal,
    temporal_query,
    temporal_key,
    temporal_value,
    temporal_output,
):
    own = VIEWS * TOKENS
    part = PART * TOKENS
    x = view_maps.reshape(own, D)
    a, b = call(
        rows_body, [(VIEWS, RADIUS, COLS, D)] * 2, 0, 40 * MIB, n_in=1,
        scratch=[pltpu.SemaphoreType.DMA((2,))],
    )(view_maps)
    slab = VIEWS * SLAB
    a = swap(a, "row", 0).reshape(slab, D)
    b = swap(b, "row", 1).reshape(slab, D)
    edge_a, edge_b = call(edges_body, [(VIEWS * EDGE, D)] * 2, 10**8, MIB, n_in=1)(x)
    edge_a, edge_b = swap(edge_a, "col", 0), swap(edge_b, "col", 1)
    (q,) = call(own_body, [(own, D)], 2 * own * D * D, 2 * MIB, n_in=3)(x, gain_spatial, spatial_query)
    corner_a, corner_b = call(corners_body, [(VIEWS * CORNER, D)] * 2, 10**8, MIB, n_in=2)(a, b)
    corner_a, corner_b = swap(corner_a, "col", 0), swap(corner_b, "col", 1)
    kv = call(
        slabs_body, [(own, D)] * 2 + [(slab, D)] * 4, 2 * (own + 2 * slab) * D * D * 2, 6 * MIB, n_in=6,
    )(x, a, b, gain_spatial, spatial_key, spatial_value)
    middles, fars, partners = [], [], []
    for c in range(CHUNKS):
        (middle,) = call(
            functools.partial(window_body, c), [(part, D)], 10**9, 8 * MIB, n_in=16,
            scratch=[pltpu.VMEM((2 * PART * SIDE, D), BF), pltpu.VMEM((2 * PART * SIDE, D), BF), pltpu.VMEM((part, D), BF)],
        )(x, q, *kv, edge_a, edge_b, corner_a, corner_b, gain_spatial, spatial_key, spatial_value, spatial_output)
        middles.append(middle)
        fars.append(across(middle, 2))
        partners.append(across(middle, 1))
    q, k, v = call(near_body, [(own, D)] * 3, 2 * own * D * D * 3, 6 * MIB, n_in=CHUNKS + 4)(
        *middles, gain_temporal, temporal_query, temporal_key, temporal_value)
    kp, vp = call(pair_body, [(own, D)] * 2, 2 * own * D * D * 2, 6 * MIB, n_in=CHUNKS + 3)(
        *partners, gain_temporal, temporal_key, temporal_value)
    keys, values = [k, kp], [v, vp]
    for c in range(CHUNKS):
        forwarded = across(fars[c], 1)
        for value, label in ((fars[c], f"far{c}"), (forwarded, f"way{c}")):
            if label != f"way{CHUNKS - 1}":
                fk, fv = call(far_body, [(part, D)] * 2, 2 * part * D * D * 2, 3 * MIB, n_in=4)(
                    value, gain_temporal, temporal_key, temporal_value)
                keys.append(fk)
                values.append(fv)
    (refined,) = call(
        views_body, [(own, D)], 10**9, 8 * MIB, n_in=CHUNKS + 1 + 2 * (2 * CHUNKS + 1) + 5,
        scratch=[pltpu.VMEM((part, D), BF), pltpu.VMEM((part, D), BF), pltpu.VMEM((own, D), BF)],
    )(*middles, q, *keys, *values, forwarded, gain_temporal, temporal_key, temporal_value, temporal_output)
    return refined.reshape(view_maps.shape)


def solution(mesh):
    return jax.shard_map(
        body,
        mesh=mesh,
        in_specs=(P("view", "row", "col", None), P(), P(), P(), P(), P(), P(), P(), P(), P(), P()),
        out_specs=P("view", "row", "col", None),
        check_vma=False,
    )
```

time: 50 us -> 47.5 us (0.950)
  the two profiles are of different devices: /device:TPU:103 before, /device:TPU:105 now
where the time goes in v3:
time: 47.5 us; the launch traced here: 47.2 us
  starting transfers between devices  27.7 us (58%)
  Pallas kernels  13.3 us (28%)
  local copies, waits for them, and re-layouts  3.68 us (8%)
  waiting for transfers between devices  2.34 us (5%)
    ppermute x6, starting transfers between devices, swap(): return lax.ppermute(value, axis, pairs + [(j, i) for i, j in pairs])  14.6 us
    ppermute x6, starting transfers between devices, across(): return lax.ppermute(value, 'view', [(i, i ^ step) for i in range(4)])  13 us
    unnamed x24, local copies, waits for them, and re-layouts  3.68 us
    pallas_call x2, Pallas kernels, body(): call(functools.partial(window_body, c), [(part, D)], 10 ** 9, 8 * MIB, n_...  3.47 us
    pallas_call x1, Pallas kernels, body(): call(views_body, [(own, D)], 10 ** 9, 8 * MIB, n_in=CHUNKS + 1 + 2 * (2 *...  3.14 us
    ppermute x6, waiting for transfers between devices, swap(): return lax.ppermute(value, axis, pairs + [(j, i) for i, j in pairs])  2.33 us
    pallas_call x1, Pallas kernels, body(): call(slabs_body, [(own, D)] * 2 + [(slab, D)] * 4, 2 * (own + 2 * slab) *...  1.82 us
    pallas_call x3, Pallas kernels, body(): call(far_body, [(part, D)] * 2, 2 * part * D * D * 2, 3 * MIB, n_in=4)  1.66 us
  transfers between devices with their start and end apart: 12, of which 1 were waited for; matrix products, arithmetic and copies ran while one was open for 0% of the time, Pallas kernels for 18%

profile of v3, /device:TPU:105, one launch (start us, length us, event | category | flops | bytes accessed | tf_op | source)
XLA Modules:
  0.0 47.2 jit_solution(3831932249616528089)
XLA Ops:
  0.0 0.0 copy-start.2
  0.0 1.0 %copy-done.2 = bf16[4,4,16,768]{3,2,1,0:T(8,128)(2,1)S(1)} copy-done((bf16[4,4,16,768]{3,2,1,0:T(8,128)(2,1)S(1)}, bf16[4,4,16,768]{3,2,1,0:T(8,128)(2,1)}, u32[]{:S(2)}) %copy-start.2) | copy-done | bytes 393240
  1.0 0.1 shard_map.110
  1.1 0.1 collective-permute-start
  1.2 5.5 %collective-permute-start.1 = (bf16[4,3,16,768]{3,2,1,0:T(8,128)(2,1)S(1)}, bf16[4,3,16,768]{3,2,1,0:T(8,128)(2,1)S(1)}, u32[]{:S(2)}, u32[]{:S(2)}) collective-permute-start(bf16[4,3,16,768]{3,2,1,0:T(8,128)(2,1)S(1)} %get-tuple-element.29), channel_id=1, source_target_pairs={{8,16},{24,32},{40,48},{16,8},{32,24},{48,40},{9,17},{25,33},{41,4... | collective-permute-start | bytes 884744 | tf_op jit(solution)/shard_map/ppermute | solution.py:272
  6.7 0.0 copy-start.5
  6.7 0.2 shard_map.112
  6.9 1.3 %collective-permute-start.2 = (bf16[48,768]{1,0:T(8,128)(2,1)S(1)}, bf16[48,768]{1,0:T(8,128)(2,1)S(1)}, u32[]{:S(2)}, u32[]{:S(2)}) collective-permute-start(bf16[48,768]{1,0:T(8,128)(2,1)S(1)} %get-tuple-element.36), channel_id=1, source_target_pairs={{0,1},{2,3},{4,5},{6,7},{1,0},{3,2},{5,4},{7,6},{8,9},{10,11},{12,... | collective-permute-start | bytes 221192 | tf_op jit(solution)/shard_map/ppermute | solution.py:272
  8.2 0.0 copy-start.3
  8.2 0.0 copy-start.4
  8.2 3.7 %collective-permute-start.3 = (bf16[48,768]{1,0:T(8,128)(2,1)S(1)}, bf16[48,768]{1,0:T(8,128)(2,1)S(1)}, u32[]{:S(2)}, u32[]{:S(2)}) collective-permute-start(bf16[48,768]{1,0:T(8,128)(2,1)S(1)} %get-tuple-element.37), channel_id=1, source_target_pairs={{1,2},{3,4},{5,6},{2,1},{4,3},{6,5},{9,10},{11,12},{13,14},{10,9},... | collective-permute-start | bytes 221192 | tf_op jit(solution)/shard_map/ppermute | solution.py:272
  11.9 0.0 copy-start.9
  11.9 1.3 %copy-done.9 = bf16[768,768]{1,0:T(8,128)(2,1)S(1)} copy-done((bf16[768,768]{1,0:T(8,128)(2,1)S(1)}, bf16[768,768]{1,0:T(8,128)(2,1)}, u32[]{:S(2)}) %copy-start.9) | copy-done | bytes 1179672
  13.2 0.0 copy-start.11
  13.2 0.7 %copy-done.11 = f32[768]{0:T(1024)S(1)} copy-done((f32[768]{0:T(1024)S(1)}, f32[768]{0:T(1024)}, u32[]{:S(2)}) %copy-start.11) | copy-done | bytes 3096
  13.9 0.6 %shard_map.109.q = bf16[256,768]{1,0:T(8,128)(2,1)S(1)} custom-call(bf16[256,768]{1,0:T(8,128)(2,1)S(1)} %bitcast.5, f32[768]{0:T(1024)S(1)} %copy-done.11, bf16[768,768]{1,0:T(8,128)(2,1)S(1)} %copy-done.9), custom_call_target="tpu_custom_call" | custom-call | flops 301989888 | bytes 2097152 | tf_op jit(solution)/shard_map/pallas_call | solution.py:304
  14.4 0.0 collective-permute-done
  14.5 0.0 collective-permute-done.1
  14.5 0.3 shard_map.113
  14.7 0.5 %collective-permute-start.4 = (bf16[72,768]{1,0:T(8,128)(2,1)S(1)}, bf16[72,768]{1,0:T(8,128)(2,1)S(1)}, u32[]{:S(2)}, u32[]{:S(2)}) collective-permute-start(bf16[72,768]{1,0:T(8,128)(2,1)S(1)} %get-tuple-element.38), channel_id=1, source_target_pairs={{0,1},{2,3},{4,5},{6,7},{1,0},{3,2},{5,4},{7,6},{8,9},{10,11},{12,... | collective-permute-start | bytes 331784 | tf_op jit(solution)/shard_map/ppermute | solution.py:272
  15.3 0.0 copy-start.6
  15.3 3.5 %collective-permute-start.5 = (bf16[72,768]{1,0:T(8,128)(2,1)S(1)}, bf16[72,768]{1,0:T(8,128)(2,1)S(1)}, u32[]{:S(2)}, u32[]{:S(2)}) collective-permute-start(bf16[72,768]{1,0:T(8,128)(2,1)S(1)} %get-tuple-element.39), channel_id=1, source_target_pairs={{1,2},{3,4},{5,6},{2,1},{4,3},{6,5},{9,10},{11,12},{13,14},{10,9},... | collective-permute-start | bytes 331784 | tf_op jit(solution)/shard_map/ppermute | solution.py:272
  18.8 0.0 copy-done.5
  18.8 0.0 copy-done.3
  18.8 0.0 copy-done.4
  18.8 1.8 %shard_map.111 = (bf16[256,768]{1,0:T(8,128)(2,1)S(1)}, bf16[256,768]{1,0:T(8,128)(2,1)S(1)}, bf16[192,768]{1,0:T(8,128)(2,1)S(1)}, bf16[192,768]{1,0:T(8,128)(2...) custom-call(bf16[256,768]{1,0:T(8,128)(2,1)S(1)} %bitcast.6, bf16[192,768]{1,0:T(8,128)(2,1)S(1)} %bitcast.10, ...), custom_call_target="tpu_custom_call" | custom-call | flops 1509949440 | bytes 6291456 | tf_op jit(solution)/shard_map/pallas_call | solution.py:307
  20.6 0.0 collective-permute-done.2.edge_a
  20.6 0.0 collective-permute-done.3.edge_b
  20.7 0.0 collective-permute-done.4.corner_a
  20.7 2.3 %collective-permute-done.5.corner_b = bf16[72,768]{1,0:T(8,128)(2,1)S(1)} collective-permute-done((bf16[72,768]{1,0:T(8,128)(2,1)S(1)}, bf16[72,768]{1,0:T(8,128)(2,1)S(1)}, u32[]{:S(2)}, u32[]{:S(2)}) %collective-permute-start.5) | collective-permute-done | bytes 110624 | tf_op jit(solution)/shard_map/ppermute | solution.py:272
  23.0 0.0 copy-done.6
  23.0 1.7 %shard_map.114.refs_0_ = bf16[128,768]{1,0:T(8,128)(2,1)S(1)} custom-call(bf16[256,768]{1,0:T(8,128)(2,1)S(1)} %bitcast.7, bf16[256,768]{1,0:T(8,128)(2,1)S(1)} %shard_map.109.q, bf16[256,768]{1,0:T(8,128)(2,1)S(1)} %get-tuple-element.30.k, bf16[256,768]{1,0:T(8,128)(2,1)S(1)} %get-tuple-element.31.v, bf16[192,768]{1,0:T(8,128)(2,1)S(1)} %get-tuple-element.32.ka, ...), custom_call_target="tpu_custom_call" | custom-call | flops 1000000000 | bytes 8388608 | tf_op jit(solution)/shard_map/pallas_call | solution.py:312
  24.7 0.0 copy-start
  24.7 0.0 copy-start.1
  24.8 0.0 copy-start.7
  24.8 0.0 copy-start.10
  24.8 2.2 %collective-permute-start.8 = (bf16[128,768]{1,0:T(8,128)(2,1)S(1)}, bf16[128,768]{1,0:T(8,128)(2,1)S(1)}, u32[]{:S(2)}, u32[]{:S(2)}) collective-permute-start(bf16[128,768]{1,0:T(8,128)(2,1)S(1)} %shard_map.114.refs_0_), channel_id=1, source_target_pairs={{0,128},{64,192},{128,0},{192,64},{1,129},{65,193},{129,1},{193,65... | collective-permute-start | bytes 589832 | tf_op jit(solution)/shard_map/ppermute | solution.py:276
  27.0 1.7 %shard_map.115.refs_1_ = bf16[128,768]{1,0:T(8,128)(2,1)S(1)} custom-call(bf16[256,768]{1,0:T(8,128)(2,1)S(1)} %bitcast.8, bf16[256,768]{1,0:T(8,128)(2,1)S(1)} %shard_map.109.q, bf16[256,768]{1,0:T(8,128)(2,1)S(1)} %get-tuple-element.30.k, bf16[256,768]{1,0:T(8,128)(2,1)S(1)} %get-tuple-element.31.v, bf16[192,768]{1,0:T(8,128)(2,1)S(1)} %get-tuple-element.32.ka, ...), custom_call_target="tpu_custom_call" | custom-call | flops 1000000000 | bytes 8388608 | tf_op jit(solution)/shard_map/pallas_call | solution.py:312
  28.7 0.9 %collective-permute-start.10 = (bf16[128,768]{1,0:T(8,128)(2,1)S(1)}, bf16[128,768]{1,0:T(8,128)(2,1)S(1)}, u32[]{:S(2)}, u32[]{:S(2)}) collective-permute-start(bf16[128,768]{1,0:T(8,128)(2,1)S(1)} %shard_map.115.refs_1_), channel_id=1, source_target_pairs={{0,128},{64,192},{128,0},{192,64},{1,129},{65,193},{129,1},{193,65... | collective-permute-start | bytes 589832 | tf_op jit(solution)/shard_map/ppermute | solution.py:276
  29.7 3.9 %collective-permute-start.6 = (bf16[128,768]{1,0:T(8,128)(2,1)S(1)}, bf16[128,768]{1,0:T(8,128)(2,1)S(1)}, u32[]{:S(2)}, u32[]{:S(2)}) collective-permute-start(bf16[128,768]{1,0:T(8,128)(2,1)S(1)} %shard_map.114.refs_0_), channel_id=1, source_target_pairs={{0,64},{64,0},{128,192},{192,128},{1,65},{65,1},{129,193},{193,129... | collective-permute-start | bytes 589832 | tf_op jit(solution)/shard_map/ppermute | solution.py:276
  33.5 0.0 collective-permute-start.7
  33.5 0.0 collective-permute-done.8.far
  33.5 3.8 %collective-permute-start.9 = (bf16[128,768]{1,0:T(8,128)(2,1)S(1)}, bf16[128,768]{1,0:T(8,128)(2,1)S(1)}, u32[]{:S(2)}, u32[]{:S(2)}) collective-permute-start(bf16[128,768]{1,0:T(8,128)(2,1)S(1)} %collective-permute-done.8.far), channel_id=1, source_target_pairs={{0,64},{64,0},{128,192},{192,128},{1,65},{65,1},{129,193},{193,129... | collective-permute-start | bytes 589832 | tf_op jit(solution)/shard_map/ppermute | solution.py:276
  37.3 0.0 collective-permute-done.10.far
  37.3 2.3 %collective-permute-start.11 = (bf16[128,768]{1,0:T(8,128)(2,1)S(1)}, bf16[128,768]{1,0:T(8,128)(2,1)S(1)}, u32[]{:S(2)}, u32[]{:S(2)}) collective-permute-start(bf16[128,768]{1,0:T(8,128)(2,1)S(1)} %collective-permute-done.10.far), channel_id=1, source_target_pairs={{0,64},{64,0},{128,192},{192,128},{1,65},{65,1},{129,193},{193,129... | collective-permute-start | bytes 589832 | tf_op jit(solution)/shard_map/ppermute | solution.py:276
  39.6 0.0 copy-done
  39.6 0.0 copy-done.1
  39.6 0.0 copy-done.7
  39.6 0.0 copy-done.10
  39.6 1.2 %shard_map.116 = (bf16[256,768]{1,0:T(8,128)(2,1)S(1)}, bf16[256,768]{1,0:T(8,128)(2,1)S(1)}, bf16[256,768]{1,0:T(8,128)(2,1)S(1)}) custom-call(bf16[128,768]{1,0:T(8,128)(2,1)S(1)} %shard_map.114.refs_0_, bf16[128,768]{1,0:T(8,128)(2,1)S(1)} %shard_map.115.refs_1_, f32[768]{0:T(1024)S(1)} %copy-done.10, bf16[768,768]{1,0:T(8,128)(2,1)S(1)} %copy-done.7, ...), custom_call_target="tpu_custom_call" | custom-call | flops 905969664 | bytes 6291456 | tf_op jit(solution)/shard_map/pallas_call | solution.py:319
  40.8 0.6 %shard_map.120 = (bf16[128,768]{1,0:T(8,128)(2,1)S(1)}, bf16[128,768]{1,0:T(8,128)(2,1)S(1)}) custom-call(bf16[128,768]{1,0:T(8,128)(2,1)S(1)} %collective-permute-done.10.far, f32[768]{0:T(1024)S(1)} %copy-done.10, bf16[768,768]{1,0:T(8,128)(2,1)S(1)} %copy-done, bf16[768,768]{1,0:T(8,128)(2,1)S(1)} %copy-done.1), custom_call_target="tpu_custom_call" | custom-call | flops 301989888 | bytes 3145728 | tf_op jit(solution)/shard_map/pallas_call | solution.py:328
  41.4 0.6 %shard_map.118 = (bf16[128,768]{1,0:T(8,128)(2,1)S(1)}, bf16[128,768]{1,0:T(8,128)(2,1)S(1)}) custom-call(bf16[128,768]{1,0:T(8,128)(2,1)S(1)} %collective-permute-done.8.far, f32[768]{0:T(1024)S(1)} %copy-done.10, bf16[768,768]{1,0:T(8,128)(2,1)S(1)} %copy-done, bf16[768,768]{1,0:T(8,128)(2,1)S(1)} %copy-done.1), custom_call_target="tpu_custom_call" | custom-call | flops 301989888 | bytes 3145728 | tf_op jit(solution)/shard_map/pallas_call | solution.py:328
  41.9 0.0 collective-permute-done.6.refs_0_
  41.9 0.0 collective-permute-done.7.refs_1_
  41.9 0.9 %shard_map.117 = (bf16[256,768]{1,0:T(8,128)(2,1)S(1)}, bf16[256,768]{1,0:T(8,128)(2,1)S(1)}) custom-call(bf16[128,768]{1,0:T(8,128)(2,1)S(1)} %collective-permute-done.6.refs_0_, bf16[128,768]{1,0:T(8,128)(2,1)S(1)} %collective-permute-done.7.refs_1_, f32[768]{0:T(1024)S(1)} %copy-done.10, bf16[768,768]{1,0:T(8,128)(2,1)S(1)} %copy-done, ...), custom_call_target="tpu_custom_call" | custom-call | flops 603979776 | bytes 6291456 | tf_op jit(solution)/shard_map/pallas_call | solution.py:321
  42.8 0.0 copy-start.8
  42.8 0.0 collective-permute-done.9.far
  42.8 0.6 %shard_map.119 = (bf16[128,768]{1,0:T(8,128)(2,1)S(1)}, bf16[128,768]{1,0:T(8,128)(2,1)S(1)}) custom-call(bf16[128,768]{1,0:T(8,128)(2,1)S(1)} %collective-permute-done.9.far, f32[768]{0:T(1024)S(1)} %copy-done.10, bf16[768,768]{1,0:T(8,128)(2,1)S(1)} %copy-done, bf16[768,768]{1,0:T(8,128)(2,1)S(1)} %copy-done.1), custom_call_target="tpu_custom_call" | custom-call | flops 301989888 | bytes 3145728 | tf_op jit(solution)/shard_map/pallas_call | solution.py:328
  43.4 0.0 collective-permute-done.11.refs_13_
  43.4 0.7 %copy-done.8 = bf16[768,768]{1,0:T(8,128)(2,1)S(1)} copy-done((bf16[768,768]{1,0:T(8,128)(2,1)S(1)}, bf16[768,768]{1,0:T(8,128)(2,1)}, u32[]{:S(2)}) %copy-start.8) | copy-done | bytes 1179672
  44.1 3.1 %shard_map.121 = bf16[256,768]{1,0:T(8,128)(2,1)} custom-call(bf16[128,768]{1,0:T(8,128)(2,1)S(1)} %shard_map.114.refs_0_, bf16[128,768]{1,0:T(8,128)(2,1)S(1)} %shard_map.115.refs_1_, bf16[256,768]{1,0:T(8,128)(2,1)S(1)} %get-tuple-element.40.refs_2_, bf16[256,768]{1,0:T(8,128)(2,1)S(1)} %get-tuple-element.41.refs_3_, ...), custom_call_target="tpu_custom_call" | custom-call | flops 1000000000 | bytes 8388608 | tf_op jit(solution)/shard_map/pallas_call | solution.py:332
Async XLA Ops:
  0.0 1.0 %copy-start.2 = (bf16[4,4,16,768]{3,2,1,0:T(8,128)(2,1)S(1)}, bf16[4,4,16,768]{3,2,1,0:T(8,128)(2,1)}, u32[]{:S(2)}) copy-start(bf16[4,4,16,768]{3,2,1,0:T(8,128)(2,1)} %maps.1) | copy-start | bytes 1179652
  1.1 13.4 %collective-permute-start = (bf16[4,3,16,768]{3,2,1,0:T(8,128)(2,1)S(1)}, bf16[4,3,16,768]{3,2,1,0:T(8,128)(2,1)S(1)}, u32[]{:S(2)}, u32[]{:S(2)}) collective-permute-start(bf16[4,3,16,768]{3,2,1,0:T(8,128)(2,1)S(1)} %get-tuple-element.28), channel_id=1, source_target_pairs={{0,8},{16,24},{32,40},{48,56},{8,0},{24,16},{40,32},{56,48},{1,9},... | collective-permute-start | bytes 884744 | tf_op jit(solution)/shard_map/ppermute | solution.py:272
  1.2 13.3 %collective-permute-start.1 = (bf16[4,3,16,768]{3,2,1,0:T(8,128)(2,1)S(1)}, bf16[4,3,16,768]{3,2,1,0:T(8,128)(2,1)S(1)}, u32[]{:S(2)}, u32[]{:S(2)}) collective-permute-start(bf16[4,3,16,768]{3,2,1,0:T(8,128)(2,1)S(1)} %get-tuple-element.29), channel_id=1, source_target_pairs={{8,16},{24,32},{40,48},{16,8},{32,24},{48,40},{9,17},{25,33},{41,4... | collective-permute-start | bytes 884744 | tf_op jit(solution)/shard_map/ppermute | solution.py:272
  6.7 12.1 %copy-start.5 = (bf16[768,768]{1,0:T(8,128)(2,1)S(1)}, bf16[768,768]{1,0:T(8,128)(2,1)}, u32[]{:S(2)}) copy-start(bf16[768,768]{1,0:T(8,128)(2,1)} %wv.8) | copy-start | bytes 3538948
  6.9 13.8 %collective-permute-start.2 = (bf16[48,768]{1,0:T(8,128)(2,1)S(1)}, bf16[48,768]{1,0:T(8,128)(2,1)S(1)}, u32[]{:S(2)}, u32[]{:S(2)}) collective-permute-start(bf16[48,768]{1,0:T(8,128)(2,1)S(1)} %get-tuple-element.36), channel_id=1, source_target_pairs={{0,1},{2,3},{4,5},{6,7},{1,0},{3,2},{5,4},{7,6},{8,9},{10,11},{12,... | collective-permute-start | bytes 221192 | tf_op jit(solution)/shard_map/ppermute | solution.py:272
  8.2 10.6 %copy-start.3 = (bf16[4,4,16,768]{3,2,1,0:T(8,128)(2,1)S(1)}, bf16[4,4,16,768]{3,2,1,0:T(8,128)(2,1)}, u32[]{:S(2)}) copy-start(bf16[4,4,16,768]{3,2,1,0:T(8,128)(2,1)} %maps.1) | copy-start | bytes 1179652
  8.2 10.6 %copy-start.4 = (bf16[768,768]{1,0:T(8,128)(2,1)S(1)}, bf16[768,768]{1,0:T(8,128)(2,1)}, u32[]{:S(2)}) copy-start(bf16[768,768]{1,0:T(8,128)(2,1)} %wk.8) | copy-start | bytes 3538948
  8.2 12.5 %collective-permute-start.3 = (bf16[48,768]{1,0:T(8,128)(2,1)S(1)}, bf16[48,768]{1,0:T(8,128)(2,1)S(1)}, u32[]{:S(2)}, u32[]{:S(2)}) collective-permute-start(bf16[48,768]{1,0:T(8,128)(2,1)S(1)} %get-tuple-element.37), channel_id=1, source_target_pairs={{1,2},{3,4},{5,6},{2,1},{4,3},{6,5},{9,10},{11,12},{13,14},{10,9},... | collective-permute-start | bytes 221192 | tf_op jit(solution)/shard_map/ppermute | solution.py:272
  11.9 1.3 %copy-start.9 = (bf16[768,768]{1,0:T(8,128)(2,1)S(1)}, bf16[768,768]{1,0:T(8,128)(2,1)}, u32[]{:S(2)}) copy-start(bf16[768,768]{1,0:T(8,128)(2,1)} %wq.1) | copy-start | bytes 3538948
  13.2 0.7 %copy-start.11 = (f32[768]{0:T(1024)S(1)}, f32[768]{0:T(1024)}, u32[]{:S(2)}) copy-start(f32[768]{0:T(1024)} %gain.10) | copy-start | bytes 9220
  14.7 5.9 %collective-permute-start.4 = (bf16[72,768]{1,0:T(8,128)(2,1)S(1)}, bf16[72,768]{1,0:T(8,128)(2,1)S(1)}, u32[]{:S(2)}, u32[]{:S(2)}) collective-permute-start(bf16[72,768]{1,0:T(8,128)(2,1)S(1)} %get-tuple-element.38), channel_id=1, source_target_pairs={{0,1},{2,3},{4,5},{6,7},{1,0},{3,2},{5,4},{7,6},{8,9},{10,11},{12,... | collective-permute-start | bytes 331784 | tf_op jit(solution)/shard_map/ppermute | solution.py:272
  15.3 7.7 %copy-start.6 = (bf16[768,768]{1,0:T(8,128)(2,1)S(1)}, bf16[768,768]{1,0:T(8,128)(2,1)}, u32[]{:S(2)}) copy-start(bf16[768,768]{1,0:T(8,128)(2,1)} %wo.3) | copy-start | bytes 3538948
  15.3 7.7 %collective-permute-start.5 = (bf16[72,768]{1,0:T(8,128)(2,1)S(1)}, bf16[72,768]{1,0:T(8,128)(2,1)S(1)}, u32[]{:S(2)}, u32[]{:S(2)}) collective-permute-start(bf16[72,768]{1,0:T(8,128)(2,1)S(1)} %get-tuple-element.39), channel_id=1, source_target_pairs={{1,2},{3,4},{5,6},{2,1},{4,3},{6,5},{9,10},{11,12},{13,14},{10,9},... | collective-permute-start | bytes 331784 | tf_op jit(solution)/shard_map/ppermute | solution.py:272
  24.7 14.8 %copy-start = (bf16[768,768]{1,0:T(8,128)(2,1)S(1)}, bf16[768,768]{1,0:T(8,128)(2,1)}, u32[]{:S(2)}) copy-start(bf16[768,768]{1,0:T(8,128)(2,1)} %refs_15_.1) | copy-start | bytes 3538948
  24.7 14.8 %copy-start.1 = (bf16[768,768]{1,0:T(8,128)(2,1)S(1)}, bf16[768,768]{1,0:T(8,128)(2,1)}, u32[]{:S(2)}) copy-start(bf16[768,768]{1,0:T(8,128)(2,1)} %refs_16_.1) | copy-start | bytes 3538948
  24.8 14.8 %copy-start.7 = (bf16[768,768]{1,0:T(8,128)(2,1)S(1)}, bf16[768,768]{1,0:T(8,128)(2,1)}, u32[]{:S(2)}) copy-start(bf16[768,768]{1,0:T(8,128)(2,1)} %refs_3_.2) | copy-start | bytes 3538948
  24.8 14.8 %copy-start.10 = (f32[768]{0:T(1024)S(1)}, f32[768]{0:T(1024)}, u32[]{:S(2)}) copy-start(f32[768]{0:T(1024)} %refs_14_.1) | copy-start | bytes 9220
  24.8 8.8 %collective-permute-start.8 = (bf16[128,768]{1,0:T(8,128)(2,1)S(1)}, bf16[128,768]{1,0:T(8,128)(2,1)S(1)}, u32[]{:S(2)}, u32[]{:S(2)}) collective-permute-start(bf16[128,768]{1,0:T(8,128)(2,1)S(1)} %shard_map.114.refs_0_), channel_id=1, source_target_pairs={{0,128},{64,192},{128,0},{192,64},{1,129},{65,193},{129,1},{193,65... | collective-permute-start | bytes 589832 | tf_op jit(solution)/shard_map/ppermute | solution.py:276
  28.7 8.6 %collective-permute-start.10 = (bf16[128,768]{1,0:T(8,128)(2,1)S(1)}, bf16[128,768]{1,0:T(8,128)(2,1)S(1)}, u32[]{:S(2)}, u32[]{:S(2)}) collective-permute-start(bf16[128,768]{1,0:T(8,128)(2,1)S(1)} %shard_map.115.refs_1_), channel_id=1, source_target_pairs={{0,128},{64,192},{128,0},{192,64},{1,129},{65,193},{129,1},{193,65... | collective-permute-start | bytes 589832 | tf_op jit(solution)/shard_map/ppermute | solution.py:276
  29.7 12.3 %collective-permute-start.6 = (bf16[128,768]{1,0:T(8,128)(2,1)S(1)}, bf16[128,768]{1,0:T(8,128)(2,1)S(1)}, u32[]{:S(2)}, u32[]{:S(2)}) collective-permute-start(bf16[128,768]{1,0:T(8,128)(2,1)S(1)} %shard_map.114.refs_0_), channel_id=1, source_target_pairs={{0,64},{64,0},{128,192},{192,128},{1,65},{65,1},{129,193},{193,129... | collective-permute-start | bytes 589832 | tf_op jit(solution)/shard_map/ppermute | solution.py:276
  33.5 8.4 %collective-permute-start.7 = (bf16[128,768]{1,0:T(8,128)(2,1)S(1)}, bf16[128,768]{1,0:T(8,128)(2,1)S(1)}, u32[]{:S(2)}, u32[]{:S(2)}) collective-permute-start(bf16[128,768]{1,0:T(8,128)(2,1)S(1)} %shard_map.115.refs_1_), channel_id=1, source_target_pairs={{0,64},{64,0},{128,192},{192,128},{1,65},{65,1},{129,193},{193,129... | collective-permute-start | bytes 589832 | tf_op jit(solution)/shard_map/ppermute | solution.py:276
  33.5 9.3 %collective-permute-start.9 = (bf16[128,768]{1,0:T(8,128)(2,1)S(1)}, bf16[128,768]{1,0:T(8,128)(2,1)S(1)}, u32[]{:S(2)}, u32[]{:S(2)}) collective-permute-start(bf16[128,768]{1,0:T(8,128)(2,1)S(1)} %collective-permute-done.8.far), channel_id=1, source_target_pairs={{0,64},{64,0},{128,192},{192,128},{1,65},{65,1},{129,193},{193,129... | collective-permute-start | bytes 589832 | tf_op jit(solution)/shard_map/ppermute | solution.py:276
  37.3 6.1 %collective-permute-start.11 = (bf16[128,768]{1,0:T(8,128)(2,1)S(1)}, bf16[128,768]{1,0:T(8,128)(2,1)S(1)}, u32[]{:S(2)}, u32[]{:S(2)}) collective-permute-start(bf16[128,768]{1,0:T(8,128)(2,1)S(1)} %collective-permute-done.10.far), channel_id=1, source_target_pairs={{0,64},{64,0},{128,192},{192,128},{1,65},{65,1},{129,193},{193,129... | collective-permute-start | bytes 589832 | tf_op jit(solution)/shard_map/ppermute | solution.py:276
  42.8 1.3 %copy-start.8 = (bf16[768,768]{1,0:T(8,128)(2,1)S(1)}, bf16[768,768]{1,0:T(8,128)(2,1)}, u32[]{:S(2)}) copy-start(bf16[768,768]{1,0:T(8,128)(2,1)} %refs_17_.1) | copy-start | bytes 3538948

commit v4 on v3

--- a/solution.py
+++ b/solution.py
@@ -14,6 +14,7 @@
 CHUNKS = 2
 D = 768
 GROUP = 4
+PAIR = 2
 LANES = GROUP * HEAD_DIM
 GROUPS = HEADS // GROUP
 ROWS = 4
@@ -119,28 +120,31 @@
         value[...] = dot(n, wv[...]).astype(BF)
 
 
-def compact(full, spread):
-    full = jnp.where(spread, full, 0.0)
-    count = full.shape[0] // GROUP
-    result = full[:count]
-    for head in range(1, GROUP):
-        result = result + full[head * count:(head + 1) * count]
-    return result
+def compact(full):
+    heads = full.shape[1] // HEAD_DIM
+    count = full.shape[0] // heads
+    tiles = []
+    for tile in range(heads // 2):
+        lanes = slice(2 * HEAD_DIM * tile, 2 * HEAD_DIM * (tile + 1))
+        low = full[2 * tile * count:(2 * tile + 1) * count, lanes]
+        high = full[(2 * tile + 1) * count:(2 * tile + 2) * count, lanes]
+        tiles.append(jnp.where(lax.broadcasted_iota(jnp.int32, low.shape, 1) < HEAD_DIM, low, high))
+    return tiles[0] if len(tiles) == 1 else jnp.concatenate(tiles, axis=1)
 
 
 def attend(q, keys, values, allowed, spread):
-    stacked = jnp.concatenate([q] * GROUP, axis=0)
+    stacked = jnp.concatenate([q] * (q.shape[1] // HEAD_DIM), axis=0)
     stacked = jnp.where(spread, stacked, jnp.zeros_like(stacked))
     scores = lax.dot_general(stacked, keys, (((1,), (1,)), ((), ())), preferred_element_type=F32)
     scores = jnp.where(allowed, scores, very_negative)
     highest = jnp.max(scores, axis=-1, keepdims=True)
     weights = jnp.exp(scores - highest)
     share = 1.0 / jnp.sum(weights, axis=-1, keepdims=True)
-    return compact(dot(weights.astype(BF), values) * share, spread).astype(BF)
-
-
-def spread_mask(count):
-    shape = (GROUP * count, LANES)
+    return compact(dot(weights.astype(BF), values) * share).astype(BF)
+
+
+def spread_mask(count, heads):
+    shape = (heads * count, heads * HEAD_DIM)
     row = lax.broadcasted_iota(jnp.int32, shape, 0)
     lane = lax.broadcasted_iota(jnp.int32, shape, 1)
     return (row // count) == (lane // HEAD_DIM)
@@ -194,7 +198,7 @@
     side_k[...] = dot(sides, wk[...]).astype(BF)
     side_v[...] = dot(sides, wv[...]).astype(BF)
     allowed = window_mask(lax.axis_index("row") * ROWS, lax.axis_index("col") * COLS)
-    spread = spread_mask(TOKENS)
+    spread = spread_mask(TOKENS, GROUP)
     for view in range(PART):
         o = slice(view * TOKENS, (view + 1) * TOKENS)
         t = slice((first + view) * TOKENS, (first + view + 1) * TOKENS)
@@ -208,8 +212,8 @@
     middle[...] = (x[first * TOKENS:(first + PART) * TOKENS].astype(F32) + dot(out[...], wo[...])).astype(BF)
 
 
-def same_place(count):
-    shape = (GROUP * TOKENS, count)
+def same_place(count, heads):
+    shape = (heads * TOKENS, count)
     i = lax.broadcasted_iota(jnp.int32, shape, 0)
     j = lax.broadcasted_iota(jnp.int32, shape, 1)
     return (i & 15) == (j & 15)
@@ -254,11 +258,11 @@
     far_body(last, gain, wk, wv, kl, vl)
     keys.append(kl)
     values.append(vl)
-    spread = spread_mask(TOKENS)
-    allowed = same_place(ALL_VIEWS * COLS)
+    spread = spread_mask(TOKENS, PAIR)
+    allowed = same_place(ALL_VIEWS * COLS, PAIR)
     for row in range(ROWS):
-        for group in range(GROUPS):
-            f = slice(group * LANES, (group + 1) * LANES)
+        for pair in range(HEADS // PAIR):
+            f = slice(pair * PAIR * HEAD_DIM, (pair + 1) * PAIR * HEAD_DIM)
             full = attend(row_of([q], row, f), row_of(keys, row, f), row_of(values, row, f), allowed, spread)
             for w in range(VIEWS):
                 out[w * TOKENS + row * COLS:w * TOKENS + (row + 1) * COLS, f] = full[w * COLS:(w + 1) * COLS]

time: 47.5 us -> 47.2 us (level)
  no operation moved by 1% of the time
where the time goes in v4:
time: 47.2 us; the launch traced here: 46.9 us
  starting transfers between devices  27.7 us (59%)
  Pallas kernels  12.9 us (27%)
  local copies, waits for them, and re-layouts  3.68 us (8%)
  waiting for transfers between devices  2.34 us (5%)
    ppermute x6, starting transfers between devices, swap(): return lax.ppermute(value, axis, pairs + [(j, i) for i, j in pairs])  14.6 us
    ppermute x6, starting transfers between devices, across(): return lax.ppermute(value, 'view', [(i, i ^ step) for i in range(4)])  13.1 us
    unnamed x24, local copies, waits for them, and re-layouts  3.68 us
    pallas_call x2, Pallas kernels, body(): call(functools.partial(window_body, c), [(part, D)], 10 ** 9, 8 * MIB, n_...  3.38 us
    pallas_call x1, Pallas kernels, body(): call(views_body, [(own, D)], 10 ** 9, 8 * MIB, n_in=CHUNKS + 1 + 2 * (2 *...  2.87 us
    ppermute x6, waiting for transfers between devices, swap(): return lax.ppermute(value, axis, pairs + [(j, i) for i, j in pairs])  2.33 us
    pallas_call x1, Pallas kernels, body(): call(slabs_body, [(own, D)] * 2 + [(slab, D)] * 4, 2 * (own + 2 * slab) *...  1.82 us
    pallas_call x3, Pallas kernels, body(): call(far_body, [(part, D)] * 2, 2 * part * D * D * 2, 3 * MIB, n_in=4)  1.66 us
  transfers between devices with their start and end apart: 12, of which 1 were waited for; matrix products, arithmetic and copies ran while one was open for 0% of the time, Pallas kernels for 18%

profile of v4, /device:TPU:105, one launch (start us, length us, event | category | flops | bytes accessed | tf_op | source)
XLA Modules:
  0.0 46.9 jit_solution(16329533795971773786)
XLA Ops:
  0.0 0.0 copy-start.2
  0.0 1.0 %copy-done.2 = bf16[4,4,16,768]{3,2,1,0:T(8,128)(2,1)S(1)} copy-done((bf16[4,4,16,768]{3,2,1,0:T(8,128)(2,1)S(1)}, bf16[4,4,16,768]{3,2,1,0:T(8,128)(2,1)}, u32[]{:S(2)}) %copy-start.2) | copy-done | bytes 393240
  1.0 0.1 shard_map.110
  1.1 0.1 collective-permute-start
  1.2 5.5 %collective-permute-start.1 = (bf16[4,3,16,768]{3,2,1,0:T(8,128)(2,1)S(1)}, bf16[4,3,16,768]{3,2,1,0:T(8,128)(2,1)S(1)}, u32[]{:S(2)}, u32[]{:S(2)}) collective-permute-start(bf16[4,3,16,768]{3,2,1,0:T(8,128)(2,1)S(1)} %get-tuple-element.29), channel_id=1, source_target_pairs={{8,16},{24,32},{40,48},{16,8},{32,24},{48,40},{9,17},{25,33},{41,4... | collective-permute-start | bytes 884744 | tf_op jit(solution)/shard_map/ppermute | solution.py:276
  6.7 0.0 copy-start.5
  6.7 0.2 shard_map.112
  6.9 1.3 %collective-permute-start.2 = (bf16[48,768]{1,0:T(8,128)(2,1)S(1)}, bf16[48,768]{1,0:T(8,128)(2,1)S(1)}, u32[]{:S(2)}, u32[]{:S(2)}) collective-permute-start(bf16[48,768]{1,0:T(8,128)(2,1)S(1)} %get-tuple-element.36), channel_id=1, source_target_pairs={{0,1},{2,3},{4,5},{6,7},{1,0},{3,2},{5,4},{7,6},{8,9},{10,11},{12,... | collective-permute-start | bytes 221192 | tf_op jit(solution)/shard_map/ppermute | solution.py:276
  8.2 0.0 copy-start.3
  8.2 0.0 copy-start.4
  8.2 3.7 %collective-permute-start.3 = (bf16[48,768]{1,0:T(8,128)(2,1)S(1)}, bf16[48,768]{1,0:T(8,128)(2,1)S(1)}, u32[]{:S(2)}, u32[]{:S(2)}) collective-permute-start(bf16[48,768]{1,0:T(8,128)(2,1)S(1)} %get-tuple-element.37), channel_id=1, source_target_pairs={{1,2},{3,4},{5,6},{2,1},{4,3},{6,5},{9,10},{11,12},{13,14},{10,9},... | collective-permute-start | bytes 221192 | tf_op jit(solution)/shard_map/ppermute | solution.py:276
  11.9 0.0 copy-start.9
  11.9 1.3 %copy-done.9 = bf16[768,768]{1,0:T(8,128)(2,1)S(1)} copy-done((bf16[768,768]{1,0:T(8,128)(2,1)S(1)}, bf16[768,768]{1,0:T(8,128)(2,1)}, u32[]{:S(2)}) %copy-start.9) | copy-done | bytes 1179672
  13.2 0.0 copy-start.11
  13.2 0.7 %copy-done.11 = f32[768]{0:T(1024)S(1)} copy-done((f32[768]{0:T(1024)S(1)}, f32[768]{0:T(1024)}, u32[]{:S(2)}) %copy-start.11) | copy-done | bytes 3096
  13.9 0.6 %shard_map.109.q = bf16[256,768]{1,0:T(8,128)(2,1)S(1)} custom-call(bf16[256,768]{1,0:T(8,128)(2,1)S(1)} %bitcast.5, f32[768]{0:T(1024)S(1)} %copy-done.11, bf16[768,768]{1,0:T(8,128)(2,1)S(1)} %copy-done.9), custom_call_target="tpu_custom_call" | custom-call | flops 301989888 | bytes 2097152 | tf_op jit(solution)/shard_map/pallas_call | solution.py:308
  14.4 0.0 collective-permute-done
  14.5 0.0 collective-permute-done.1
  14.5 0.3 shard_map.113
  14.7 0.5 %collective-permute-start.4 = (bf16[72,768]{1,0:T(8,128)(2,1)S(1)}, bf16[72,768]{1,0:T(8,128)(2,1)S(1)}, u32[]{:S(2)}, u32[]{:S(2)}) collective-permute-start(bf16[72,768]{1,0:T(8,128)(2,1)S(1)} %get-tuple-element.38), channel_id=1, source_target_pairs={{0,1},{2,3},{4,5},{6,7},{1,0},{3,2},{5,4},{7,6},{8,9},{10,11},{12,... | collective-permute-start | bytes 331784 | tf_op jit(solution)/shard_map/ppermute | solution.py:276
  15.3 0.0 copy-start.6
  15.3 3.5 %collective-permute-start.5 = (bf16[72,768]{1,0:T(8,128)(2,1)S(1)}, bf16[72,768]{1,0:T(8,128)(2,1)S(1)}, u32[]{:S(2)}, u32[]{:S(2)}) collective-permute-start(bf16[72,768]{1,0:T(8,128)(2,1)S(1)} %get-tuple-element.39), channel_id=1, source_target_pairs={{1,2},{3,4},{5,6},{2,1},{4,3},{6,5},{9,10},{11,12},{13,14},{10,9},... | collective-permute-start | bytes 331784 | tf_op jit(solution)/shard_map/ppermute | solution.py:276
  18.8 0.0 copy-done.5
  18.8 0.0 copy-done.3
  18.8 0.0 copy-done.4
  18.8 1.8 %shard_map.111 = (bf16[256,768]{1,0:T(8,128)(2,1)S(1)}, bf16[256,768]{1,0:T(8,128)(2,1)S(1)}, bf16[192,768]{1,0:T(8,128)(2,1)S(1)}, bf16[192,768]{1,0:T(8,128)(2...) custom-call(bf16[256,768]{1,0:T(8,128)(2,1)S(1)} %bitcast.6, bf16[192,768]{1,0:T(8,128)(2,1)S(1)} %bitcast.10, ...), custom_call_target="tpu_custom_call" | custom-call | flops 1509949440 | bytes 6291456 | tf_op jit(solution)/shard_map/pallas_call | solution.py:311
  20.6 0.0 collective-permute-done.2.edge_a
  20.6 0.0 collective-permute-done.3.edge_b
  20.7 0.0 collective-permute-done.4.corner_a
  20.7 2.3 %collective-permute-done.5.corner_b = bf16[72,768]{1,0:T(8,128)(2,1)S(1)} collective-permute-done((bf16[72,768]{1,0:T(8,128)(2,1)S(1)}, bf16[72,768]{1,0:T(8,128)(2,1)S(1)}, u32[]{:S(2)}, u32[]{:S(2)}) %collective-permute-start.5) | collective-permute-done | bytes 110624 | tf_op jit(solution)/shard_map/ppermute | solution.py:276
  23.0 0.0 copy-done.6
  23.0 1.7 %shard_map.114.refs_0_ = bf16[128,768]{1,0:T(8,128)(2,1)S(1)} custom-call(bf16[256,768]{1,0:T(8,128)(2,1)S(1)} %bitcast.7, bf16[256,768]{1,0:T(8,128)(2,1)S(1)} %shard_map.109.q, bf16[256,768]{1,0:T(8,128)(2,1)S(1)} %get-tuple-element.30.k, bf16[256,768]{1,0:T(8,128)(2,1)S(1)} %get-tuple-element.31.v, bf16[192,768]{1,0:T(8,128)(2,1)S(1)} %get-tuple-element.32.ka, ...), custom_call_target="tpu_custom_call" | custom-call | flops 1000000000 | bytes 8388608 | tf_op jit(solution)/shard_map/pallas_call | solution.py:316
  24.7 0.0 copy-start
  24.7 0.0 copy-start.1
  24.7 0.0 copy-start.7
  24.7 0.0 copy-start.10
  24.7 2.2 %collective-permute-start.8 = (bf16[128,768]{1,0:T(8,128)(2,1)S(1)}, bf16[128,768]{1,0:T(8,128)(2,1)S(1)}, u32[]{:S(2)}, u32[]{:S(2)}) collective-permute-start(bf16[128,768]{1,0:T(8,128)(2,1)S(1)} %shard_map.114.refs_0_), channel_id=1, source_target_pairs={{0,128},{64,192},{128,0},{192,64},{1,129},{65,193},{129,1},{193,65... | collective-permute-start | bytes 589832 | tf_op jit(solution)/shard_map/ppermute | solution.py:280
  26.9 1.7 %shard_map.115.refs_1_ = bf16[128,768]{1,0:T(8,128)(2,1)S(1)} custom-call(bf16[256,768]{1,0:T(8,128)(2,1)S(1)} %bitcast.8, bf16[256,768]{1,0:T(8,128)(2,1)S(1)} %shard_map.109.q, bf16[256,768]{1,0:T(8,128)(2,1)S(1)} %get-tuple-element.30.k, bf16[256,768]{1,0:T(8,128)(2,1)S(1)} %get-tuple-element.31.v, bf16[192,768]{1,0:T(8,128)(2,1)S(1)} %get-tuple-element.32.ka, ...), custom_call_target="tpu_custom_call" | custom-call | flops 1000000000 | bytes 8388608 | tf_op jit(solution)/shard_map/pallas_call | solution.py:316
  28.6 1.0 %collective-permute-start.10 = (bf16[128,768]{1,0:T(8,128)(2,1)S(1)}, bf16[128,768]{1,0:T(8,128)(2,1)S(1)}, u32[]{:S(2)}, u32[]{:S(2)}) collective-permute-start(bf16[128,768]{1,0:T(8,128)(2,1)S(1)} %shard_map.115.refs_1_), channel_id=1, source_target_pairs={{0,128},{64,192},{128,0},{192,64},{1,129},{65,193},{129,1},{193,65... | collective-permute-start | bytes 589832 | tf_op jit(solution)/shard_map/ppermute | solution.py:280
  29.6 3.9 %collective-permute-start.6 = (bf16[128,768]{1,0:T(8,128)(2,1)S(1)}, bf16[128,768]{1,0:T(8,128)(2,1)S(1)}, u32[]{:S(2)}, u32[]{:S(2)}) collective-permute-start(bf16[128,768]{1,0:T(8,128)(2,1)S(1)} %shard_map.114.refs_0_), channel_id=1, source_target_pairs={{0,64},{64,0},{128,192},{192,128},{1,65},{65,1},{129,193},{193,129... | collective-permute-start | bytes 589832 | tf_op jit(solution)/shard_map/ppermute | solution.py:280
  33.4 0.0 collective-permute-start.7
  33.5 0.0 collective-permute-done.8.far
  33.5 3.9 %collective-permute-start.9 = (bf16[128,768]{1,0:T(8,128)(2,1)S(1)}, bf16[128,768]{1,0:T(8,128)(2,1)S(1)}, u32[]{:S(2)}, u32[]{:S(2)}) collective-permute-start(bf16[128,768]{1,0:T(8,128)(2,1)S(1)} %collective-permute-done.8.far), channel_id=1, source_target_pairs={{0,64},{64,0},{128,192},{192,128},{1,65},{65,1},{129,193},{193,129... | collective-permute-start | bytes 589832 | tf_op jit(solution)/shard_map/ppermute | solution.py:280
  37.3 0.0 collective-permute-done.10.far
  37.3 2.2 %collective-permute-start.11 = (bf16[128,768]{1,0:T(8,128)(2,1)S(1)}, bf16[128,768]{1,0:T(8,128)(2,1)S(1)}, u32[]{:S(2)}, u32[]{:S(2)}) collective-permute-start(bf16[128,768]{1,0:T(8,128)(2,1)S(1)} %collective-permute-done.10.far), channel_id=1, source_target_pairs={{0,64},{64,0},{128,192},{192,128},{1,65},{65,1},{129,193},{193,129... | collective-permute-start | bytes 589832 | tf_op jit(solution)/shard_map/ppermute | solution.py:280
  39.5 0.0 copy-done
  39.5 0.0 copy-done.1
  39.5 0.0 copy-done.7
  39.5 0.0 copy-done.10
  39.5 1.2 %shard_map.116 = (bf16[256,768]{1,0:T(8,128)(2,1)S(1)}, bf16[256,768]{1,0:T(8,128)(2,1)S(1)}, bf16[256,768]{1,0:T(8,128)(2,1)S(1)}) custom-call(bf16[128,768]{1,0:T(8,128)(2,1)S(1)} %shard_map.114.refs_0_, bf16[128,768]{1,0:T(8,128)(2,1)S(1)} %shard_map.115.refs_1_, f32[768]{0:T(1024)S(1)} %copy-done.10, bf16[768,768]{1,0:T(8,128)(2,1)S(1)} %copy-done.7, ...), custom_call_target="tpu_custom_call" | custom-call | flops 905969664 | bytes 6291456 | tf_op jit(solution)/shard_map/pallas_call | solution.py:323
  40.7 0.6 %shard_map.120 = (bf16[128,768]{1,0:T(8,128)(2,1)S(1)}, bf16[128,768]{1,0:T(8,128)(2,1)S(1)}) custom-call(bf16[128,768]{1,0:T(8,128)(2,1)S(1)} %collective-permute-done.10.far, f32[768]{0:T(1024)S(1)} %copy-done.10, bf16[768,768]{1,0:T(8,128)(2,1)S(1)} %copy-done, bf16[768,768]{1,0:T(8,128)(2,1)S(1)} %copy-done.1), custom_call_target="tpu_custom_call" | custom-call | flops 301989888 | bytes 3145728 | tf_op jit(solution)/shard_map/pallas_call | solution.py:332
  41.3 0.6 %shard_map.118 = (bf16[128,768]{1,0:T(8,128)(2,1)S(1)}, bf16[128,768]{1,0:T(8,128)(2,1)S(1)}) custom-call(bf16[128,768]{1,0:T(8,128)(2,1)S(1)} %collective-permute-done.8.far, f32[768]{0:T(1024)S(1)} %copy-done.10, bf16[768,768]{1,0:T(8,128)(2,1)S(1)} %copy-done, bf16[768,768]{1,0:T(8,128)(2,1)S(1)} %copy-done.1), custom_call_target="tpu_custom_call" | custom-call | flops 301989888 | bytes 3145728 | tf_op jit(solution)/shard_map/pallas_call | solution.py:332
  41.9 0.0 collective-permute-done.6.refs_0_
  41.9 0.0 collective-permute-done.7.refs_1_
  41.9 0.9 %shard_map.117 = (bf16[256,768]{1,0:T(8,128)(2,1)S(1)}, bf16[256,768]{1,0:T(8,128)(2,1)S(1)}) custom-call(bf16[128,768]{1,0:T(8,128)(2,1)S(1)} %collective-permute-done.6.refs_0_, bf16[128,768]{1,0:T(8,128)(2,1)S(1)} %collective-permute-done.7.refs_1_, f32[768]{0:T(1024)S(1)} %copy-done.10, bf16[768,768]{1,0:T(8,128)(2,1)S(1)} %copy-done, ...), custom_call_target="tpu_custom_call" | custom-call | flops 603979776 | bytes 6291456 | tf_op jit(solution)/shard_map/pallas_call | solution.py:325
  42.8 0.0 copy-start.8
  42.8 0.0 collective-permute-done.9.far
  42.8 0.6 %shard_map.119 = (bf16[128,768]{1,0:T(8,128)(2,1)S(1)}, bf16[128,768]{1,0:T(8,128)(2,1)S(1)}) custom-call(bf16[128,768]{1,0:T(8,128)(2,1)S(1)} %collective-permute-done.9.far, f32[768]{0:T(1024)S(1)} %copy-done.10, bf16[768,768]{1,0:T(8,128)(2,1)S(1)} %copy-done, bf16[768,768]{1,0:T(8,128)(2,1)S(1)} %copy-done.1), custom_call_target="tpu_custom_call" | custom-call | flops 301989888 | bytes 3145728 | tf_op jit(solution)/shard_map/pallas_call | solution.py:332
  43.4 0.0 collective-permute-done.11.refs_13_
  43.4 0.7 %copy-done.8 = bf16[768,768]{1,0:T(8,128)(2,1)S(1)} copy-done((bf16[768,768]{1,0:T(8,128)(2,1)S(1)}, bf16[768,768]{1,0:T(8,128)(2,1)}, u32[]{:S(2)}) %copy-start.8) | copy-done | bytes 1179672
  44.0 2.9 %shard_map.121 = bf16[256,768]{1,0:T(8,128)(2,1)} custom-call(bf16[128,768]{1,0:T(8,128)(2,1)S(1)} %shard_map.114.refs_0_, bf16[128,768]{1,0:T(8,128)(2,1)S(1)} %shard_map.115.refs_1_, bf16[256,768]{1,0:T(8,128)(2,1)S(1)} %get-tuple-element.40.refs_2_, bf16[256,768]{1,0:T(8,128)(2,1)S(1)} %get-tuple-element.41.refs_3_, ...), custom_call_target="tpu_custom_call" | custom-call | flops 1000000000 | bytes 8388608 | tf_op jit(solution)/shard_map/pallas_call | solution.py:336
Async XLA Ops:
  0.0 1.0 %copy-start.2 = (bf16[4,4,16,768]{3,2,1,0:T(8,128)(2,1)S(1)}, bf16[4,4,16,768]{3,2,1,0:T(8,128)(2,1)}, u32[]{:S(2)}) copy-start(bf16[4,4,16,768]{3,2,1,0:T(8,128)(2,1)} %maps.1) | copy-start | bytes 1179652
  1.1 13.4 %collective-permute-start = (bf16[4,3,16,768]{3,2,1,0:T(8,128)(2,1)S(1)}, bf16[4,3,16,768]{3,2,1,0:T(8,128)(2,1)S(1)}, u32[]{:S(2)}, u32[]{:S(2)}) collective-permute-start(bf16[4,3,16,768]{3,2,1,0:T(8,128)(2,1)S(1)} %get-tuple-element.28), channel_id=1, source_target_pairs={{0,8},{16,24},{32,40},{48,56},{8,0},{24,16},{40,32},{56,48},{1,9},... | collective-permute-start | bytes 884744 | tf_op jit(solution)/shard_map/ppermute | solution.py:276
  1.2 13.3 %collective-permute-start.1 = (bf16[4,3,16,768]{3,2,1,0:T(8,128)(2,1)S(1)}, bf16[4,3,16,768]{3,2,1,0:T(8,128)(2,1)S(1)}, u32[]{:S(2)}, u32[]{:S(2)}) collective-permute-start(bf16[4,3,16,768]{3,2,1,0:T(8,128)(2,1)S(1)} %get-tuple-element.29), channel_id=1, source_target_pairs={{8,16},{24,32},{40,48},{16,8},{32,24},{48,40},{9,17},{25,33},{41,4... | collective-permute-start | bytes 884744 | tf_op jit(solution)/shard_map/ppermute | solution.py:276
  6.7 12.1 %copy-start.5 = (bf16[768,768]{1,0:T(8,128)(2,1)S(1)}, bf16[768,768]{1,0:T(8,128)(2,1)}, u32[]{:S(2)}) copy-start(bf16[768,768]{1,0:T(8,128)(2,1)} %wv.8) | copy-start | bytes 3538948
  6.9 13.8 %collective-permute-start.2 = (bf16[48,768]{1,0:T(8,128)(2,1)S(1)}, bf16[48,768]{1,0:T(8,128)(2,1)S(1)}, u32[]{:S(2)}, u32[]{:S(2)}) collective-permute-start(bf16[48,768]{1,0:T(8,128)(2,1)S(1)} %get-tuple-element.36), channel_id=1, source_target_pairs={{0,1},{2,3},{4,5},{6,7},{1,0},{3,2},{5,4},{7,6},{8,9},{10,11},{12,... | collective-permute-start | bytes 221192 | tf_op jit(solution)/shard_map/ppermute | solution.py:276
  8.2 10.6 %copy-start.3 = (bf16[4,4,16,768]{3,2,1,0:T(8,128)(2,1)S(1)}, bf16[4,4,16,768]{3,2,1,0:T(8,128)(2,1)}, u32[]{:S(2)}) copy-start(bf16[4,4,16,768]{3,2,1,0:T(8,128)(2,1)} %maps.1) | copy-start | bytes 1179652
  8.2 10.6 %copy-start.4 = (bf16[768,768]{1,0:T(8,128)(2,1)S(1)}, bf16[768,768]{1,0:T(8,128)(2,1)}, u32[]{:S(2)}) copy-start(bf16[768,768]{1,0:T(8,128)(2,1)} %wk.8) | copy-start | bytes 3538948
  8.2 12.5 %collective-permute-start.3 = (bf16[48,768]{1,0:T(8,128)(2,1)S(1)}, bf16[48,768]{1,0:T(8,128)(2,1)S(1)}, u32[]{:S(2)}, u32[]{:S(2)}) collective-permute-start(bf16[48,768]{1,0:T(8,128)(2,1)S(1)} %get-tuple-element.37), channel_id=1, source_target_pairs={{1,2},{3,4},{5,6},{2,1},{4,3},{6,5},{9,10},{11,12},{13,14},{10,9},... | collective-permute-start | bytes 221192 | tf_op jit(solution)/shard_map/ppermute | solution.py:276
  11.9 1.3 %copy-start.9 = (bf16[768,768]{1,0:T(8,128)(2,1)S(1)}, bf16[768,768]{1,0:T(8,128)(2,1)}, u32[]{:S(2)}) copy-start(bf16[768,768]{1,0:T(8,128)(2,1)} %wq.1) | copy-start | bytes 3538948
  13.2 0.7 %copy-start.11 = (f32[768]{0:T(1024)S(1)}, f32[768]{0:T(1024)}, u32[]{:S(2)}) copy-start(f32[768]{0:T(1024)} %gain.10) | copy-start | bytes 9220
  14.7 5.9 %collective-permute-start.4 = (bf16[72,768]{1,0:T(8,128)(2,1)S(1)}, bf16[72,768]{1,0:T(8,128)(2,1)S(1)}, u32[]{:S(2)}, u32[]{:S(2)}) collective-permute-start(bf16[72,768]{1,0:T(8,128)(2,1)S(1)} %get-tuple-element.38), channel_id=1, source_target_pairs={{0,1},{2,3},{4,5},{6,7},{1,0},{3,2},{5,4},{7,6},{8,9},{10,11},{12,... | collective-permute-start | bytes 331784 | tf_op jit(solution)/shard_map/ppermute | solution.py:276
  15.3 7.7 %copy-start.6 = (bf16[768,768]{1,0:T(8,128)(2,1)S(1)}, bf16[768,768]{1,0:T(8,128)(2,1)}, u32[]{:S(2)}) copy-start(bf16[768,768]{1,0:T(8,128)(2,1)} %wo.3) | copy-start | bytes 3538948
  15.3 7.7 %collective-permute-start.5 = (bf16[72,768]{1,0:T(8,128)(2,1)S(1)}, bf16[72,768]{1,0:T(8,128)(2,1)S(1)}, u32[]{:S(2)}, u32[]{:S(2)}) collective-permute-start(bf16[72,768]{1,0:T(8,128)(2,1)S(1)} %get-tuple-element.39), channel_id=1, source_target_pairs={{1,2},{3,4},{5,6},{2,1},{4,3},{6,5},{9,10},{11,12},{13,14},{10,9},... | collective-permute-start | bytes 331784 | tf_op jit(solution)/shard_map/ppermute | solution.py:276
  24.7 14.8 %copy-start = (bf16[768,768]{1,0:T(8,128)(2,1)S(1)}, bf16[768,768]{1,0:T(8,128)(2,1)}, u32[]{:S(2)}) copy-start(bf16[768,768]{1,0:T(8,128)(2,1)} %refs_15_.1) | copy-start | bytes 3538948
  24.7 14.8 %copy-start.1 = (bf16[768,768]{1,0:T(8,128)(2,1)S(1)}, bf16[768,768]{1,0:T(8,128)(2,1)}, u32[]{:S(2)}) copy-start(bf16[768,768]{1,0:T(8,128)(2,1)} %refs_16_.1) | copy-start | bytes 3538948
  24.7 14.8 %copy-start.7 = (bf16[768,768]{1,0:T(8,128)(2,1)S(1)}, bf16[768,768]{1,0:T(8,128)(2,1)}, u32[]{:S(2)}) copy-start(bf16[768,768]{1,0:T(8,128)(2,1)} %refs_3_.2) | copy-start | bytes 3538948
  24.7 14.8 %copy-start.10 = (f32[768]{0:T(1024)S(1)}, f32[768]{0:T(1024)}, u32[]{:S(2)}) copy-start(f32[768]{0:T(1024)} %refs_14_.1) | copy-start | bytes 9220
  24.7 8.7 %collective-permute-start.8 = (bf16[128,768]{1,0:T(8,128)(2,1)S(1)}, bf16[128,768]{1,0:T(8,128)(2,1)S(1)}, u32[]{:S(2)}, u32[]{:S(2)}) collective-permute-start(bf16[128,768]{1,0:T(8,128)(2,1)S(1)} %shard_map.114.refs_0_), channel_id=1, source_target_pairs={{0,128},{64,192},{128,0},{192,64},{1,129},{65,193},{129,1},{193,65... | collective-permute-start | bytes 589832 | tf_op jit(solution)/shard_map/ppermute | solution.py:280
  28.6 8.7 %collective-permute-start.10 = (bf16[128,768]{1,0:T(8,128)(2,1)S(1)}, bf16[128,768]{1,0:T(8,128)(2,1)S(1)}, u32[]{:S(2)}, u32[]{:S(2)}) collective-permute-start(bf16[128,768]{1,0:T(8,128)(2,1)S(1)} %shard_map.115.refs_1_), channel_id=1, source_target_pairs={{0,128},{64,192},{128,0},{192,64},{1,129},{65,193},{129,1},{193,65... | collective-permute-start | bytes 589832 | tf_op jit(solution)/shard_map/ppermute | solution.py:280
  29.6 12.3 %collective-permute-start.6 = (bf16[128,768]{1,0:T(8,128)(2,1)S(1)}, bf16[128,768]{1,0:T(8,128)(2,1)S(1)}, u32[]{:S(2)}, u32[]{:S(2)}) collective-permute-start(bf16[128,768]{1,0:T(8,128)(2,1)S(1)} %shard_map.114.refs_0_), channel_id=1, source_target_pairs={{0,64},{64,0},{128,192},{192,128},{1,65},{65,1},{129,193},{193,129... | collective-permute-start | bytes 589832 | tf_op jit(solution)/shard_map/ppermute | solution.py:280
  33.4 8.4 %collective-permute-start.7 = (bf16[128,768]{1,0:T(8,128)(2,1)S(1)}, bf16[128,768]{1,0:T(8,128)(2,1)S(1)}, u32[]{:S(2)}, u32[]{:S(2)}) collective-permute-start(bf16[128,768]{1,0:T(8,128)(2,1)S(1)} %shard_map.115.refs_1_), channel_id=1, source_target_pairs={{0,64},{64,0},{128,192},{192,128},{1,65},{65,1},{129,193},{193,129... | collective-permute-start | bytes 589832 | tf_op jit(solution)/shard_map/ppermute | solution.py:280
  33.5 9.3 %collective-permute-start.9 = (bf16[128,768]{1,0:T(8,128)(2,1)S(1)}, bf16[128,768]{1,0:T(8,128)(2,1)S(1)}, u32[]{:S(2)}, u32[]{:S(2)}) collective-permute-start(bf16[128,768]{1,0:T(8,128)(2,1)S(1)} %collective-permute-done.8.far), channel_id=1, source_target_pairs={{0,64},{64,0},{128,192},{192,128},{1,65},{65,1},{129,193},{193,129... | collective-permute-start | bytes 589832 | tf_op jit(solution)/shard_map/ppermute | solution.py:280
  37.3 6.0 %collective-permute-start.11 = (bf16[128,768]{1,0:T(8,128)(2,1)S(1)}, bf16[128,768]{1,0:T(8,128)(2,1)S(1)}, u32[]{:S(2)}, u32[]{:S(2)}) collective-permute-start(bf16[128,768]{1,0:T(8,128)(2,1)S(1)} %collective-permute-done.10.far), channel_id=1, source_target_pairs={{0,64},{64,0},{128,192},{192,128},{1,65},{65,1},{129,193},{193,129... | collective-permute-start | bytes 589832 | tf_op jit(solution)/shard_map/ppermute | solution.py:280
  42.8 1.3 %copy-start.8 = (bf16[768,768]{1,0:T(8,128)(2,1)S(1)}, bf16[768,768]{1,0:T(8,128)(2,1)}, u32[]{:S(2)}) copy-start(bf16[768,768]{1,0:T(8,128)(2,1)} %refs_17_.1) | copy-start | bytes 3538948
